TPU v7x, 512 devices: a whole 4x4x16 slice. The times are simulated.
512 devices in a mesh: gx: 8 (over z_hi, y), gy: 4 (over x), gz: 16 (over z_lo, core).
Axes of the slice: x: 4, y: 4, z: 16 (z_hi: 2, z_lo: 8; z = z_hi * 8 + z_lo), core: 2. Of those that a mesh axis runs over, the one named last changes fastest.
Arguments:
- right_side: float32 [64, 32, 16, 4096], P(None, 'gx', 'gy', 'gz'), may hold values from -6 to 6
- stiffness: float32 [32, 16, 4096], P('gx', 'gy', 'gz'), may hold values from 0.35 to 2.5
- reaction: float32 [32, 16, 4096], P('gx', 'gy', 'gz'), may hold values from 0.1 to 1
- deflation: bfloat16 [128, 32, 16, 4096], P(None, 'gx', 'gy', 'gz'), may hold values from -0.09375 to 0.09375
- coarse_blocks: bfloat16 [512, 7, 128, 128], P(('gx', 'gy', 'gz')), may hold values from -3 to 4, as said below
- row_owner: int32 [512], P(('gx', 'gy', 'gz')), may hold values from 0 to 15, as said below
- neighbours: int32 [512, 6], P(('gx', 'gy', 'gz')), may hold values from 0 to 15, as said below
Outputs:
- solution: float32 [64, 32, 16, 4096], P(None, 'gx', 'gy', 'gz')
- residual: float32 [64, 32, 16, 4096], P(None, 'gx', 'gy', 'gz')
Inputs may be any that keep to these rules, and one draw needn't show every extreme that they name: `row_owner`: each entry is a multiple of 3. For the block row at position c of its line, entries 0 and 1 are (c - 1) and (c + 1) modulo 16, its neighbours along the third dimension; entries 2 to 5 are any positions in the line. `coarse_blocks`: blocks of order one; the diagonal block is near 2 times the identity.
All inputs are finite; a program needn't handle non-finite values.
Results may differ from a plain program's by a relative error of at most 0.013.
Values may be sent and summed in bfloat16 or wider, within the bound.
A program may use at most 64 MiB of HBM per device.

v0:
```python
import jax
import jax.numpy as jnp
from jax import lax
from jax.sharding import PartitionSpec as P

ITERS = 2
CHEB = 2


RELAX_WEIGHT = 0.8
CENTRE_VALUE = 2.0
HALF_WIDTH = 1.0


def extended(block, sides, width):
    for axis, dim in sides:
        count = lax.axis_size(axis)
        forward = [(i, i + 1) for i in range(count - 1)]
        backward = [(target, source) for source, target in forward]
        low = lax.ppermute(
            lax.slice_in_dim(block, block.shape[dim] - width, None, axis=dim), axis, forward
        )
        high = lax.ppermute(lax.slice_in_dim(block, 0, width, axis=dim), axis, backward)
        block = jnp.concatenate([low, block, high], axis=dim)
    return block


def stencil_sum(padded):
    return (
        padded[:, 2:, 1:-1, 1:-1]
        + padded[:, :-2, 1:-1, 1:-1]
        + padded[:, 1:-1, 2:, 1:-1]
        + padded[:, 1:-1, :-2, 1:-1]
        + padded[:, 1:-1, 1:-1, 2:]
        + padded[:, 1:-1, 1:-1, :-2]
    )


def finish_operator(padded, values, stiffness, reaction):
    centre = padded[:, 1:-1, 1:-1, 1:-1]
    return stiffness * (6.0 * centre - stencil_sum(padded)) + reaction * values


def apply_local(values, stiffness, reaction):
    padded = jnp.pad(stiffness * values, ((0, 0), (1, 1), (1, 1), (1, 1)))
    return finish_operator(padded, values, stiffness, reaction)


def chebyshev(coarse_rhs, apply_coarse):
    target = coarse_rhs.astype(jnp.float32)
    ratio_now = HALF_WIDTH / CENTRE_VALUE
    direction = target / CENTRE_VALUE
    coarse = direction
    for step_index in range(CHEB):
        ratio_next = 1.0 / (2.0 * CENTRE_VALUE / HALF_WIDTH - ratio_now)
        misfit = target - apply_coarse(coarse.astype(jnp.bfloat16))
        direction = ratio_next * ratio_now * direction + 2.0 * ratio_next / HALF_WIDTH * misfit
        coarse = coarse + direction
        ratio_now = ratio_next
    return coarse.astype(jnp.bfloat16)


def local(right_side, stiffness, reaction, deflation, coarse_blocks, row_owner, neighbours):
    count_rhs = right_side.shape[0]
    cells = deflation.shape[1] * deflation.shape[2] * deflation.shape[3]
    vectors = deflation.reshape(deflation.shape[0], cells)
    diagonal = 6.0 * stiffness * stiffness + reaction
    line_places = jnp.arange(lax.axis_size("gz"))
    line_owner = lax.all_gather(row_owner, "gz", axis=0, tiled=True)
    chosen = (
        (neighbours[0][:, None] == line_places[None, :]) & (line_owner[None, :] == row_owner[0])
    ).astype(jnp.bfloat16)
    own_blocks = coarse_blocks[0]

    def apply_coarse(values):
        line_values = lax.all_gather(values[None], "gz", axis=0, tiled=True)
        picked = jnp.einsum(
            "jq,qrk->jrk", chosen, line_values, preferred_element_type=jnp.float32
        ).astype(jnp.bfloat16)
        return jnp.dot(values, own_blocks[0], preferred_element_type=jnp.float32) + jnp.einsum(
            "jrk,jkm->rm", picked, own_blocks[1:], preferred_element_type=jnp.float32
        )

    solution = jnp.zeros_like(right_side)
    residual = right_side
    for iteration in range(ITERS):
        smooth = RELAX_WEIGHT * residual / diagonal
        smooth = (
            smooth + RELAX_WEIGHT * (residual - apply_local(smooth, stiffness, reaction)) / diagonal
        )
        rounded = residual.astype(jnp.bfloat16).reshape(count_rhs, cells)
        coarse_rhs = jnp.einsum(
            "rc,kc->rk", rounded, vectors, preferred_element_type=jnp.float32
        ).astype(jnp.bfloat16)
        coarse = chebyshev(coarse_rhs, apply_coarse)
        prolong = jnp.dot(coarse, vectors, preferred_element_type=jnp.float32).reshape(
            right_side.shape
        )
        update = smooth + prolong
        padded = extended(stiffness * update, (("gx", 1), ("gy", 2), ("gz", 3)), 1)
        applied = finish_operator(padded, update, stiffness, reaction)
        solution = solution + update
        residual = residual - applied
    return (solution, residual)


def solution(mesh):
    return jax.shard_map(
        local,
        mesh=mesh,
        in_specs=(
            P(None, "gx", "gy", "gz"),
            P("gx", "gy", "gz"),
            P("gx", "gy", "gz"),
            P(None, "gx", "gy", "gz"),
            P(("gx", "gy", "gz"), None, None, None),
            P(("gx", "gy", "gz")),
            P(("gx", "gy", "gz"), None),
        ),
        out_specs=(P(None, "gx", "gy", "gz"), P(None, "gx", "gy", "gz")),
        check_vma=False,
    )
```

profile of v0, /device:TPU:25, one launch (start us, length us, event | category | flops | bytes accessed | tf_op | source)
XLA Modules:
  0.0 304.1 jit_solution(5431531434829326783)
XLA Ops:
  3.4 16.6 %all-reduce.2 = s32[16]{0:T(128)S(1)} all-reduce(s32[16]{0:T(128)S(1)} %dynamic-update-slice), channel_id=1, replica_groups=mesh['gx'=8,'gy'=4,'gz'=16] {'gz'}, use_global_device_ids=true, to_apply=%add.2 | all-reduce | flops 16 | bytes 128
  23.6 29.9 %all-gather = bf16[1024,128]{1,0:T(8,128)(2,1)S(1)} all-gather(bf16[64,128]{1,0:T(8,128)(2,1)S(1)} %get-tuple-element.22), channel_id=2, replica_groups=mesh['gx'=8,'gy'=4,'gz'=16] {'gz'}, dimensions={0}, use_global_device_ids=true | all-gather | bytes 278528 | tf_op jit(solution)/shard_map/all_gather | solution.py:76
  54.9 28.6 %all-gather.1 = bf16[1024,128]{1,0:T(8,128)(2,1)} all-gather(bf16[64,128]{1,0:T(8,128)(2,1)S(1)} %get-tuple-element.24), channel_id=3, replica_groups=mesh['gx'=8,'gy'=4,'gz'=16] {'gz'}, dimensions={0}, use_global_device_ids=true | all-gather | bytes 278528 | tf_op jit(solution)/shard_map/all_gather | solution.py:76
  88.6 5.9 %broadcast_multiply_fusion.1 = (f32[64,4,4,256]{3,0,2,1:T(8,128)S(1)}, f32[64,4,4,256]{3,0,2,1:T(8,128)}) fusion(f32[4,4,256]{2,1,0:T(4,128)S(1)} %copy-done.14, bf16[4,4,256,128]{3,2,1,0:T(8,128)(2,1)S(1)} %bitcast.143, f32[64,128]{1,0:T(8,128)S(1)} %get-tuple-element.23, f32[64,128]{1,0:T(8,128)S(1)} %copy-done.16, ...), kind=kOutput, calls=%fused_computation.135 | convolution fusion | flops 84484096 | bytes 5685248 | tf_op jit(solution)/shard_map/dot_general | solution.py:96
  94.5 10.7 %collective-permute-start.1 = (f32[64,1,4,256]{3,0,2,1:T(8,128)S(1)}, f32[64,1,4,256]{3,0,2,1:T(8,128)S(1)}, u32[]{:S(2)}, u32[]{:S(2)}) collective-permute-start(f32[64,1,4,256]{3,0,2,1:T(8,128)S(1)} %get-tuple-element.20), channel_id=1, source_target_pairs={{0,64},{64,128},{128,192},{192,256},{256,320},{320,384},{384,448},... | collective-permute-start | bytes 786440 | tf_op jit(solution)/shard_map/ppermute | solution.py:20
  107.2 3.5 %collective-permute-done.1 = f32[64,1,4,256]{3,0,2,1:T(8,128)S(1)} collective-permute-done((f32[64,1,4,256]{3,0,2,1:T(8,128)S(1)}, f32[64,1,4,256]{3,0,2,1:T(8,128)S(1)}, u32[]{:S(2)}, u32[]{:S(2)}) %collective-permute-start.1) | collective-permute-done | bytes 262176 | tf_op jit(solution)/shard_map/ppermute | solution.py:20
  110.8 14.7 %collective-permute-done = f32[64,1,4,256]{3,0,2,1:T(8,128)S(1)} collective-permute-done((f32[64,1,4,256]{3,0,2,1:T(8,128)S(1)}, f32[64,1,4,256]{3,0,2,1:T(8,128)S(1)}, u32[]{:S(2)}, u32[]{:S(2)}) %collective-permute-start) | collective-permute-done | bytes 262176 | tf_op jit(solution)/shard_map/ppermute | solution.py:23
  125.5 3.1 %collective-permute-start.3 = (f32[64,6,1,256]{3,0,2,1:T(8,128)S(1)}, f32[64,6,1,256]{3,0,2,1:T(8,128)S(1)}, u32[]{:S(2)}, u32[]{:S(2)}) collective-permute-start(f32[64,6,1,256]{3,0,2,1:T(8,128)S(1)} %get-tuple-element.14), channel_id=1, source_target_pairs={{0,16},{16,32},{32,48},{1,17},{17,33},{33,49},{2,18},{18,34},{34,5... | collective-permute-start | bytes 1179656 | tf_op jit(solution)/shard_map/ppermute | solution.py:20
  129.9 5.7 %collective-permute-done.3 = f32[64,6,1,256]{3,0,2,1:T(8,128)S(1)} collective-permute-done((f32[64,6,1,256]{3,0,2,1:T(8,128)S(1)}, f32[64,6,1,256]{3,0,2,1:T(8,128)S(1)}, u32[]{:S(2)}, u32[]{:S(2)}) %collective-permute-start.3) | collective-permute-done | bytes 393248 | tf_op jit(solution)/shard_map/ppermute | solution.py:20
  135.7 3.9 %collective-permute-done.2 = f32[64,6,1,256]{3,0,2,1:T(8,128)S(1)} collective-permute-done((f32[64,6,1,256]{3,0,2,1:T(8,128)S(1)}, f32[64,6,1,256]{3,0,2,1:T(8,128)S(1)}, u32[]{:S(2)}, u32[]{:S(2)}) %collective-permute-start.2) | collective-permute-done | bytes 393248 | tf_op jit(solution)/shard_map/ppermute | solution.py:23
  143.8 4.5 %collective-permute-start.4 = (f32[64,6,6,1]{0,3,2,1:T(1,128)S(1)}, f32[64,6,6,1]{0,3,2,1:T(1,128)S(1)}, u32[]{:S(2)}, u32[]{:S(2)}) collective-permute-start(f32[64,6,6,1]{0,3,2,1:T(1,128)S(1)} %copy.23), channel_id=1, source_target_pairs={{1,0},{2,1},{3,2},{4,3},{5,4},{6,5},{7,6},{8,7},{9,8},{10,9},{11,1... | collective-permute-start | bytes 27656 | tf_op jit(solution)/shard_map/ppermute | solution.py:23
  149.9 13.2 %collective-permute-start.5 = (f32[64,6,6,1]{0,3,2,1:T(1,128)S(1)}, f32[64,6,6,1]{0,3,2,1:T(1,128)S(1)}, u32[]{:S(2)}, u32[]{:S(2)}) collective-permute-start(f32[64,6,6,1]{0,3,2,1:T(1,128)S(1)} %copy.25), channel_id=1, source_target_pairs={{0,1},{1,2},{2,3},{3,4},{4,5},{5,6},{6,7},{7,8},{8,9},{9,10},{10,1... | collective-permute-start | bytes 27656 | tf_op jit(solution)/shard_map/ppermute | solution.py:20
  166.1 3.9 %fusion.70 = (f32[64,4,4,256]{3,0,2,1:T(8,128)}, f32[64,4,4,256]{3,0,2,1:T(8,128)S(1)}) fusion(f32[4,4,256]{2,1,0:T(4,128)S(1)} %copy-done.14, f32[4,4,256]{2,1,0:T(4,128)S(1)} %fusion.110, f32[64,4,4,256]{3,0,2,1:T(8,128)} %get-tuple-element.27, f32[4,4,256]{2,1,0:T(4,128)S(1)} %copy-done.15, f32[64,6,1,256]{3,0,2,1:T(8,128)} %copy-done.6, ...), kind=kLoop, calls=%fused_computation.130 | loop fusion | flops 8388608 | bytes 6621184 | tf_op jit(solution)/shard_map/mul | solution.py:45
  170.9 28.0 %all-gather.2 = bf16[1024,128]{1,0:T(8,128)(2,1)S(1)} all-gather(bf16[64,128]{1,0:T(8,128)(2,1)S(1)} %get-tuple-element.28), channel_id=4, replica_groups=mesh['gx'=8,'gy'=4,'gz'=16] {'gz'}, dimensions={0}, use_global_device_ids=true | all-gather | bytes 278528 | tf_op jit(solution)/shard_map/all_gather | solution.py:76
  199.5 26.4 %all-gather.3 = bf16[1024,128]{1,0:T(8,128)(2,1)S(1)} all-gather(bf16[64,128]{1,0:T(8,128)(2,1)S(1)} %get-tuple-element.30), channel_id=5, replica_groups=mesh['gx'=8,'gy'=4,'gz'=16] {'gz'}, dimensions={0}, use_global_device_ids=true | all-gather | bytes 278528 | tf_op jit(solution)/shard_map/all_gather | solution.py:76
  227.5 6.2 %broadcast_multiply_fusion = (f32[64,4,4,256]{3,0,2,1:T(8,128)S(1)}, f32[64,4,4,256]{3,0,2,1:T(8,128)}, f32[64,4,4,256]{3,0,2,1:T(8,128)}) fusion(f32[4,4,256]{2,1,0:T(4,128)S(1)} %copy-done.14, f32[64,4,4,256]{3,0,2,1:T(8,128)S(1)} %copy-done.12, bf16[4,4,256,128]{3,2,1,0:T(8,128)(2,1)} %bitcast.144, f32[64,128]{1,0:T(8,128)S(1)} %get-tuple-element.29, ...), kind=kOutput, calls=%fused_computation.134 | convolution fusion | flops 84746240 | bytes 7782400 | tf_op jit(solution)/shard_map/dot_general | solution.py:96
  235.6 3.4 %collective-permute-start.6 = (f32[64,1,4,256]{3,0,2,1:T(8,128)S(1)}, f32[64,1,4,256]{3,0,2,1:T(8,128)S(1)}, u32[]{:S(2)}, u32[]{:S(2)}) collective-permute-start(f32[64,1,4,256]{3,0,2,1:T(8,128)S(1)} %get-tuple-element.17), channel_id=1, source_target_pairs={{64,0},{128,64},{192,128},{256,192},{320,256},{384,320},{448,384},... | collective-permute-start | bytes 786440 | tf_op jit(solution)/shard_map/ppermute | solution.py:23
  239.0 4.3 %collective-permute-done.7 = f32[64,1,4,256]{3,0,2,1:T(8,128)S(1)} collective-permute-done((f32[64,1,4,256]{3,0,2,1:T(8,128)S(1)}, f32[64,1,4,256]{3,0,2,1:T(8,128)S(1)}, u32[]{:S(2)}, u32[]{:S(2)}) %collective-permute-start.7) | collective-permute-done | bytes 262176 | tf_op jit(solution)/shard_map/ppermute | solution.py:20
  243.3 12.8 %collective-permute-done.6 = f32[64,1,4,256]{3,0,2,1:T(8,128)S(1)} collective-permute-done((f32[64,1,4,256]{3,0,2,1:T(8,128)S(1)}, f32[64,1,4,256]{3,0,2,1:T(8,128)S(1)}, u32[]{:S(2)}, u32[]{:S(2)}) %collective-permute-start.6) | collective-permute-done | bytes 262176 | tf_op jit(solution)/shard_map/ppermute | solution.py:23
  256.1 3.1 %collective-permute-start.9 = (f32[64,6,1,256]{3,0,2,1:T(8,128)S(1)}, f32[64,6,1,256]{3,0,2,1:T(8,128)S(1)}, u32[]{:S(2)}, u32[]{:S(2)}) collective-permute-start(f32[64,6,1,256]{3,0,2,1:T(8,128)S(1)} %get-tuple-element.12), channel_id=1, source_target_pairs={{0,16},{16,32},{32,48},{1,17},{17,33},{33,49},{2,18},{18,34},{34,5... | collective-permute-start | bytes 1179656 | tf_op jit(solution)/shard_map/ppermute | solution.py:20
  260.7 5.8 %collective-permute-done.9 = f32[64,6,1,256]{3,0,2,1:T(8,128)S(1)} collective-permute-done((f32[64,6,1,256]{3,0,2,1:T(8,128)S(1)}, f32[64,6,1,256]{3,0,2,1:T(8,128)S(1)}, u32[]{:S(2)}, u32[]{:S(2)}) %collective-permute-start.9) | collective-permute-done | bytes 393248 | tf_op jit(solution)/shard_map/ppermute | solution.py:20
  266.6 3.9 %collective-permute-done.8 = f32[64,6,1,256]{3,0,2,1:T(8,128)S(1)} collective-permute-done((f32[64,6,1,256]{3,0,2,1:T(8,128)S(1)}, f32[64,6,1,256]{3,0,2,1:T(8,128)S(1)}, u32[]{:S(2)}, u32[]{:S(2)}) %collective-permute-start.8) | collective-permute-done | bytes 393248 | tf_op jit(solution)/shard_map/ppermute | solution.py:23
  275.2 4.2 %collective-permute-start.10 = (f32[64,6,6,1]{0,3,2,1:T(1,128)}, f32[64,6,6,1]{0,3,2,1:T(1,128)}, u32[]{:S(2)}, u32[]{:S(2)}) collective-permute-start(f32[64,6,6,1]{0,3,2,1:T(1,128)} %copy.29), channel_id=1, source_target_pairs={{1,0},{2,1},{3,2},{4,3},{5,4},{6,5},{7,6},{8,7},{9,8},{10,9},{11,1... | collective-permute-start | bytes 27656 | tf_op jit(solution)/shard_map/ppermute | solution.py:23
  280.3 12.8 %collective-permute-start.11 = (f32[64,6,6,1]{0,3,2,1:T(1,128)}, f32[64,6,6,1]{0,3,2,1:T(1,128)}, u32[]{:S(2)}, u32[]{:S(2)}) collective-permute-start(f32[64,6,6,1]{0,3,2,1:T(1,128)} %copy.31), channel_id=1, source_target_pairs={{0,1},{1,2},{2,3},{3,4},{4,5},{5,6},{6,7},{7,8},{8,9},{9,10},{10,1... | collective-permute-start | bytes 27656 | tf_op jit(solution)/shard_map/ppermute | solution.py:20
  (88 shorter events, 47.3 us)
Async XLA Ops:
  0.6 53.0 %copy-start.9 = (bf16[1,7,128,128]{3,2,1,0:T(8,128)(2,1)S(1)}, bf16[1,7,128,128]{3,2,1,0:T(8,128)(2,1)}, u32[]{:S(2)}) copy-start(bf16[1,7,128,128]{3,2,1,0:T(8,128)(2,1)} %param.11) | copy-start | bytes 688132
  0.6 53.1 %copy-start.17 = (s32[1,6]{1,0:T(1,128)S(1)}, s32[1,6]{1,0:T(1,128)}, u32[]{:S(2)}) copy-start(s32[1,6]{1,0:T(1,128)} %param.13) | copy-start | bytes 76
  19.9 63.6 %copy-start.1 = (bf16[128,4,4,256]{3,2,1,0:T(4,128)(2,1)S(1)}, bf16[128,4,4,256]{3,2,1,0:T(4,128)(2,1)}, u32[]{:S(2)}) copy-start(bf16[128,4,4,256]{3,2,1,0:T(4,128)(2,1)} %param.10) | copy-start | bytes 3145732
  23.6 62.6 %copy-start.14 = (f32[4,4,256]{2,1,0:T(4,128)S(1)}, f32[4,4,256]{2,1,0:T(4,128)}, u32[]{:S(2)}) copy-start(f32[4,4,256]{2,1,0:T(4,128)} %param.8) | copy-start | bytes 49156
  23.6 62.6 %copy-start.15 = (f32[4,4,256]{2,1,0:T(4,128)S(1)}, f32[4,4,256]{2,1,0:T(4,128)}, u32[]{:S(2)}) copy-start(f32[4,4,256]{2,1,0:T(4,128)} %param.9) | copy-start | bytes 49156
  23.6 62.6 %copy-start = (f32[64,4,4,256]{3,2,1,0:T(4,128)S(1)}, f32[64,4,4,256]{3,2,1,0:T(4,128)}, u32[]{:S(2)}) copy-start(f32[64,4,4,256]{3,2,1,0:T(4,128)} %param.7) | copy-start | bytes 3145732
  53.7 145.2 %copy-start.19 = (pred[16]{0:T(512)(128)(4,1)}, pred[16]{0:T(512)(128)(4,1)S(1)}, u32[]{:S(2)}) copy-start(pred[16]{0:T(512)(128)(4,1)S(1)} %broadcast_compare_fusion) | copy-start | bytes 52
  94.5 16.2 %collective-permute-start.1 = (f32[64,1,4,256]{3,0,2,1:T(8,128)S(1)}, f32[64,1,4,256]{3,0,2,1:T(8,128)S(1)}, u32[]{:S(2)}, u32[]{:S(2)}) collective-permute-start(f32[64,1,4,256]{3,0,2,1:T(8,128)S(1)} %get-tuple-element.20), channel_id=1, source_target_pairs={{0,64},{64,128},{128,192},{192,256},{256,320},{320,384},{384,448},... | collective-permute-start | bytes 786440 | tf_op jit(solution)/shard_map/ppermute | solution.py:20
  105.3 20.1 %collective-permute-start = (f32[64,1,4,256]{3,0,2,1:T(8,128)S(1)}, f32[64,1,4,256]{3,0,2,1:T(8,128)S(1)}, u32[]{:S(2)}, u32[]{:S(2)}) collective-permute-start(f32[64,1,4,256]{3,0,2,1:T(8,128)S(1)} %get-tuple-element.21), channel_id=1, source_target_pairs={{64,0},{128,64},{192,128},{256,192},{320,256},{384,320},{448,384},... | collective-permute-start | bytes 786440 | tf_op jit(solution)/shard_map/ppermute | solution.py:23
  125.4 14.4 %copy-start.4 = (f32[64,1,4,256]{3,0,2,1:T(8,128)}, f32[64,1,4,256]{3,0,2,1:T(8,128)S(1)}, u32[]{:S(2)}) copy-start(f32[64,1,4,256]{3,0,2,1:T(8,128)S(1)} %collective-permute-done) | copy-start | bytes 786436
  125.5 10.2 %collective-permute-start.3 = (f32[64,6,1,256]{3,0,2,1:T(8,128)S(1)}, f32[64,6,1,256]{3,0,2,1:T(8,128)S(1)}, u32[]{:S(2)}, u32[]{:S(2)}) collective-permute-start(f32[64,6,1,256]{3,0,2,1:T(8,128)S(1)} %get-tuple-element.14), channel_id=1, source_target_pairs={{0,16},{16,32},{32,48},{1,17},{17,33},{33,49},{2,18},{18,34},{34,5... | collective-permute-start | bytes 1179656 | tf_op jit(solution)/shard_map/ppermute | solution.py:20
  128.6 10.9 %collective-permute-start.2 = (f32[64,6,1,256]{3,0,2,1:T(8,128)S(1)}, f32[64,6,1,256]{3,0,2,1:T(8,128)S(1)}, u32[]{:S(2)}, u32[]{:S(2)}) collective-permute-start(f32[64,6,1,256]{3,0,2,1:T(8,128)S(1)} %get-tuple-element.15), channel_id=1, source_target_pairs={{16,0},{32,16},{48,32},{17,1},{33,17},{49,33},{18,2},{34,18},{50,3... | collective-permute-start | bytes 1179656 | tf_op jit(solution)/shard_map/ppermute | solution.py:23
  143.8 19.3 %collective-permute-start.4 = (f32[64,6,6,1]{0,3,2,1:T(1,128)S(1)}, f32[64,6,6,1]{0,3,2,1:T(1,128)S(1)}, u32[]{:S(2)}, u32[]{:S(2)}) collective-permute-start(f32[64,6,6,1]{0,3,2,1:T(1,128)S(1)} %copy.23), channel_id=1, source_target_pairs={{1,0},{2,1},{3,2},{4,3},{5,4},{6,5},{7,6},{8,7},{9,8},{10,9},{11,1... | collective-permute-start | bytes 27656 | tf_op jit(solution)/shard_map/ppermute | solution.py:23
  149.9 14.7 %collective-permute-start.5 = (f32[64,6,6,1]{0,3,2,1:T(1,128)S(1)}, f32[64,6,6,1]{0,3,2,1:T(1,128)S(1)}, u32[]{:S(2)}, u32[]{:S(2)}) collective-permute-start(f32[64,6,6,1]{0,3,2,1:T(1,128)S(1)} %copy.25), channel_id=1, source_target_pairs={{0,1},{1,2},{2,3},{3,4},{4,5},{5,6},{6,7},{7,8},{8,9},{9,10},{10,1... | collective-permute-start | bytes 27656 | tf_op jit(solution)/shard_map/ppermute | solution.py:20
  170.0 55.9 %copy-start.18 = (s32[1,6]{1,0:T(1,128)S(1)}, s32[1,6]{1,0:T(1,128)}, u32[]{:S(2)}) copy-start(s32[1,6]{1,0:T(1,128)} %param.13) | copy-start | bytes 76
  170.0 57.4 %copy-start.11 = (bf16[1,7,128,128]{3,2,1,0:T(8,128)(2,1)S(1)}, bf16[1,7,128,128]{3,2,1,0:T(8,128)(2,1)}, u32[]{:S(2)}) copy-start(bf16[1,7,128,128]{3,2,1,0:T(8,128)(2,1)} %param.11) | copy-start | bytes 688132
  170.0 57.4 %copy-start.12 = (f32[64,4,4,256]{3,0,2,1:T(8,128)S(1)}, f32[64,4,4,256]{3,0,2,1:T(8,128)}, u32[]{:S(2)}) copy-start(f32[64,4,4,256]{3,0,2,1:T(8,128)} %get-tuple-element.27) | copy-start | bytes 3145732
  233.7 9.6 %collective-permute-start.7 = (f32[64,1,4,256]{3,0,2,1:T(8,128)S(1)}, f32[64,1,4,256]{3,0,2,1:T(8,128)S(1)}, u32[]{:S(2)}, u32[]{:S(2)}) collective-permute-start(f32[64,1,4,256]{3,0,2,1:T(8,128)S(1)} %get-tuple-element.16), channel_id=1, source_target_pairs={{0,64},{64,128},{128,192},{192,256},{256,320},{320,384},{384,448},... | collective-permute-start | bytes 786440 | tf_op jit(solution)/shard_map/ppermute | solution.py:20
  235.6 20.4 %collective-permute-start.6 = (f32[64,1,4,256]{3,0,2,1:T(8,128)S(1)}, f32[64,1,4,256]{3,0,2,1:T(8,128)S(1)}, u32[]{:S(2)}, u32[]{:S(2)}) collective-permute-start(f32[64,1,4,256]{3,0,2,1:T(8,128)S(1)} %get-tuple-element.17), channel_id=1, source_target_pairs={{64,0},{128,64},{192,128},{256,192},{320,256},{384,320},{448,384},... | collective-permute-start | bytes 786440 | tf_op jit(solution)/shard_map/ppermute | solution.py:23
  256.0 14.4 %copy-start.3 = (f32[64,1,4,256]{3,0,2,1:T(8,128)}, f32[64,1,4,256]{3,0,2,1:T(8,128)S(1)}, u32[]{:S(2)}) copy-start(f32[64,1,4,256]{3,0,2,1:T(8,128)S(1)} %collective-permute-done.6) | copy-start | bytes 786436
  256.1 10.4 %collective-permute-start.9 = (f32[64,6,1,256]{3,0,2,1:T(8,128)S(1)}, f32[64,6,1,256]{3,0,2,1:T(8,128)S(1)}, u32[]{:S(2)}, u32[]{:S(2)}) collective-permute-start(f32[64,6,1,256]{3,0,2,1:T(8,128)S(1)} %get-tuple-element.12), channel_id=1, source_target_pairs={{0,16},{16,32},{32,48},{1,17},{17,33},{33,49},{2,18},{18,34},{34,5... | collective-permute-start | bytes 1179656 | tf_op jit(solution)/shard_map/ppermute | solution.py:20
  259.3 11.2 %collective-permute-start.8 = (f32[64,6,1,256]{3,0,2,1:T(8,128)S(1)}, f32[64,6,1,256]{3,0,2,1:T(8,128)S(1)}, u32[]{:S(2)}, u32[]{:S(2)}) collective-permute-start(f32[64,6,1,256]{3,0,2,1:T(8,128)S(1)} %get-tuple-element.13), channel_id=1, source_target_pairs={{16,0},{32,16},{48,32},{17,1},{33,17},{49,33},{18,2},{34,18},{50,3... | collective-permute-start | bytes 1179656 | tf_op jit(solution)/shard_map/ppermute | solution.py:23
  275.2 20.9 %collective-permute-start.10 = (f32[64,6,6,1]{0,3,2,1:T(1,128)}, f32[64,6,6,1]{0,3,2,1:T(1,128)}, u32[]{:S(2)}, u32[]{:S(2)}) collective-permute-start(f32[64,6,6,1]{0,3,2,1:T(1,128)} %copy.29), channel_id=1, source_target_pairs={{1,0},{2,1},{3,2},{4,3},{5,4},{6,5},{7,6},{8,7},{9,8},{10,9},{11,1... | collective-permute-start | bytes 27656 | tf_op jit(solution)/shard_map/ppermute | solution.py:23
  280.3 16.9 %collective-permute-start.11 = (f32[64,6,6,1]{0,3,2,1:T(1,128)}, f32[64,6,6,1]{0,3,2,1:T(1,128)}, u32[]{:S(2)}, u32[]{:S(2)}) collective-permute-start(f32[64,6,6,1]{0,3,2,1:T(1,128)} %copy.31), channel_id=1, source_target_pairs={{0,1},{1,2},{2,3},{3,4},{4,5},{5,6},{6,7},{7,8},{8,9},{9,10},{10,1... | collective-permute-start | bytes 27656 | tf_op jit(solution)/shard_map/ppermute | solution.py:20
  (8 other events, 28.4 us)
where the time goes:
time: 305 us; the launch traced here: 304 us
  blocking collectives  129 us (42%)
  starting transfers between devices  61.6 us (20%)
  waiting for transfers between devices  54.5 us (18%)
  local copies, waits for them, and re-layouts  25.6 us (8%)
  matrix products  20.4 us (7%)
  other arithmetic  10.7 us (4%)
    all_gather x4, blocking collectives, apply_coarse(): line_values = lax.all_gather(values[None], 'gz', axis=0, tiled=True)  113 us
    ppermute x6, starting transfers between devices, extended(): lax.ppermute(lax.slice_in_dim(block, block.shape[dim] - width, None, axis...  44.9 us
    ppermute x6, waiting for transfers between devices, extended(): lax.ppermute(lax.slice_in_dim(block, 0, width, axis=dim), axis, backward)  35.1 us
    ppermute x6, waiting for transfers between devices, extended(): lax.ppermute(lax.slice_in_dim(block, block.shape[dim] - width, None, axis...  19.4 us
    ppermute x6, starting transfers between devices, extended(): lax.ppermute(lax.slice_in_dim(block, 0, width, axis=dim), axis, backward)  16.7 us
    unnamed x1, blocking collectives  16.6 us
    dot_general x2, matrix products, local(): jnp.dot(coarse, vectors, preferred_element_type=jnp.float32)  12.1 us
    unnamed x45, local copies, waits for them, and re-layouts  7.86 us
  transfers between devices with their start and end apart: 12, of which 8 were waited for; matrix products, arithmetic and copies ran while one was open for 3% of the time, Pallas kernels for 0%

commit v1 on v0

v1 whole, which is shorter than its diff:
```python
import functools

import jax
import jax.numpy as jnp
from jax import lax
from jax.experimental import pallas as pl
from jax.experimental.pallas import tpu as pltpu
from jax.sharding import PartitionSpec as P

ITERS = 2
CHEB = 2

RELAX_WEIGHT = 0.8
CENTRE_VALUE = 2.0
HALF_WIDTH = 1.0

MESH = pl.DeviceIdType.MESH
F32 = jnp.float32
BF16 = jnp.bfloat16


def flip(place, bits):
    bit = 1
    while bit <= bits:
        if bits & bit:
            place = place + bit - 2 * bit * ((place // bit) % 2)
        bit *= 2
    return place


def kernel(
    sizes,
    r_ref,
    s_ref,
    react_ref,
    z_ref,
    b_ref,
    owner_ref,
    near_ref,
    sol_ref,
    res_ref,
    coef,
    wpad,
    smooth,
    blocks,
    owners,
    line0,
    line1,
    line2,
    line3,
    xsend,
    xrecv,
    ysend,
    yrecv,
    zsend,
    zrecv,
    owner_send_sem,
    owner_recv_sem,
    line_send_sem,
    line_recv_sem,
    face_send_sem,
    face_recv_sem,
):
    n_gx, n_gy, n_gz, cx, cy, cz = sizes
    rows = r_ref.shape[0]
    n_chips = n_gz // 2
    pad_y = cy + 2
    a, b, g = lax.axis_index("gx"), lax.axis_index("gy"), lax.axis_index("gz")
    chip, core = g // 2, g % 2
    partner = chip * 2 + 1 - core
    line = (line0, line1, line2, line3)

    def at_line(place):
        return {"gz": place}

    barrier = pltpu.get_barrier_semaphore()
    for step in range(1, n_gz):
        pl.semaphore_signal(
            barrier, inc=1, device_id=at_line((g + step) % n_gz), device_id_type=MESH
        )
    places = (("gx", a, n_gx), ("gy", b, n_gy))
    for name, place, count in places:

        @pl.when(place > 0)
        def _():
            pl.semaphore_signal(
                barrier, inc=1, device_id={name: place - 1}, device_id_type=MESH
            )

        @pl.when(place < count - 1)
        def _():
            pl.semaphore_signal(
                barrier, inc=1, device_id={name: place + 1}, device_id_type=MESH
            )

    stiff = s_ref[...]
    diagonal = 6.0 * stiff * stiff + react_ref[...]
    relax = RELAX_WEIGHT / diagonal
    coef[0] = stiff
    coef[1] = diagonal
    coef[2] = (2.0 - RELAX_WEIGHT) * relax
    coef[3] = stiff * relax

    lane = lax.broadcasted_iota(jnp.int32, (rows, cz), 1)
    narrow = lax.broadcasted_iota(jnp.int32, (rows, 128), 1)

    def cols(j):
        return pl.ds(pl.multiple_of(j * cz, cz), cz)

    def padded(j):
        x, y = j // cy, j % cy
        return ((x + 1) * pad_y + y + 1) * cz

    def pcols(offset):
        return pl.ds(pl.multiple_of(offset, cz), cz)

    def row(which, j):
        return coef[which, pl.ds(j, 1), :]

    def beside(offset):
        centre = wpad[:, pcols(offset)]
        total = wpad[:, pcols(offset + pad_y * cz)] + wpad[:, pcols(offset - pad_y * cz)]
        total = total + wpad[:, pcols(offset + cz)] + wpad[:, pcols(offset - cz)]
        total = total + jnp.where(lane == cz - 1, 0.0, pltpu.roll(centre, cz - 1, 1))
        return total + jnp.where(lane == 0, 0.0, pltpu.roll(centre, 1, 1))

    def each(first, count, body):
        def step(i, carry):
            body(first + i)
            return carry

        lax.fori_loop(0, count, step, 0)

    zero_row = jnp.zeros((rows, pad_y * cz), F32)
    wpad[:, pl.ds(0, pad_y * cz)] = zero_row
    wpad[:, pl.ds((cx + 1) * pad_y * cz, pad_y * cz)] = zero_row
    for x in range(cx):
        wpad[:, pl.ds((x + 1) * pad_y * cz, cz)] = jnp.zeros((rows, cz), F32)
        wpad[:, pl.ds(((x + 2) * pad_y - 1) * cz, cz)] = jnp.zeros((rows, cz), F32)

    faces = (("gx", a, n_gx, xrecv), ("gy", b, n_gy, yrecv), ("gz", g, n_gz, zrecv))
    for it in range(ITERS):
        for name, place, count, recv in faces:

            @pl.when(place == 0)
            def _():
                recv[it, 0] = jnp.zeros(recv.shape[2:], recv.dtype)

            @pl.when(place == count - 1)
            def _():
                recv[it, 1] = jnp.zeros(recv.shape[2:], recv.dtype)

    def restrict(field):
        width = cy * cz
        total = jnp.zeros((rows, z_ref.shape[0]), F32)
        for x in range(cx):
            part = pl.ds(x * width, width)
            total = total + lax.dot_general(
                field[:, part].astype(BF16),
                z_ref[:, part],
                (((1,), (1,)), ((), ())),
                preferred_element_type=F32,
            )
        return total.astype(BF16)

    def line_copy(turn, slot, sem, target):
        return pltpu.make_async_remote_copy(
            src_ref=line[turn].at[slot],
            dst_ref=line[turn].at[slot],
            send_sem=line_send_sem.at[turn, sem],
            recv_sem=line_recv_sem.at[turn, slot],
            device_id=at_line(target),
            device_id_type=MESH,
        )

    def line_start(turn, value):
        line[turn][g] = value
        for bits in range(n_chips - 1, 0, -1):
            line_copy(turn, g, bits, flip(chip, bits) * 2 + core).start()
        line_copy(turn, g, 0, partner).start()

    def line_finish(turn):
        for bits in range(1, n_chips):
            source = flip(chip, bits) * 2 + core
            line_copy(turn, source, 0, partner).wait_recv()
            line_copy(turn, source, n_chips + bits, partner).start()
        line_copy(turn, partner, 0, partner).wait_recv()
        for bits in range(1, n_chips):
            source = flip(chip, bits) * 2 + 1 - core
            line_copy(turn, source, 0, partner).wait_recv()

    def line_drain(turn):
        for sem in range(n_chips):
            line_copy(turn, g, sem, partner).wait_send()
        for bits in range(1, n_chips):
            line_copy(turn, g, n_chips + bits, partner).wait_send()

    def face_copy(it, axis, side, send, recv, name, target):
        return pltpu.make_async_remote_copy(
            src_ref=send.at[it, side],
            dst_ref=recv.at[it, 1 - side],
            send_sem=face_send_sem.at[it, axis, side],
            recv_sem=face_recv_sem.at[it, axis, 1 - side],
            device_id={name: target},
            device_id_type=MESH,
        )

    exchange = (
        (0, "gx", a, n_gx, xsend, xrecv),
        (1, "gy", b, n_gy, ysend, yrecv),
        (2, "gz", g, n_gz, zsend, zrecv),
    )

    def face_start(it, which):
        axis, name, place, count, send, recv = exchange[which]

        @pl.when(place > 0)
        def _():
            face_copy(it, axis, 0, send, recv, name, place - 1).start()

        @pl.when(place < count - 1)
        def _():
            face_copy(it, axis, 1, send, recv, name, place + 1).start()

    def face_wait(it, which):
        axis, name, place, count, send, recv = exchange[which]

        @pl.when(place > 0)
        def _():
            face_copy(it, axis, 1, send, recv, name, place - 1).wait_recv()

        @pl.when(place < count - 1)
        def _():
            face_copy(it, axis, 0, send, recv, name, place + 1).wait_recv()

    def face_drain(it, which):
        axis, name, place, count, send, recv = exchange[which]

        @pl.when(place > 0)
        def _():
            face_copy(it, axis, 0, send, recv, name, place - 1).wait_send()

        @pl.when(place < count - 1)
        def _():
            face_copy(it, axis, 1, send, recv, name, place + 1).wait_send()

    def relaxed(field):
        def scale(j):
            wpad[:, pcols(padded(j))] = row(3, j) * field[:, cols(j)]

        def combine(j):
            smooth[:, cols(j)] = row(2, j) * field[:, cols(j)] + row(3, j) * beside(padded(j))

        each(0, cx * cy, scale)
        each(0, cx * cy, combine)

    def apply_coarse(turn, value):
        picked = [value] + [line[turn][near_ref[0, k]] for k in range(6)]
        return jnp.dot(
            jnp.concatenate(picked, axis=1), blocks[...], preferred_element_type=F32
        )

    def owner_copy(target):
        return pltpu.make_async_remote_copy(
            src_ref=owners.at[g],
            dst_ref=owners.at[g],
            send_sem=owner_send_sem,
            recv_sem=owner_recv_sem,
            device_id=at_line(target),
            device_id_type=MESH,
        )

    owners[g] = jnp.full((1, 128), owner_ref[0], jnp.int32)
    for it in range(ITERS):
        field = r_ref if it == 0 else res_ref
        coarse_rhs = restrict(field)
        if it == 0:
            peers = n_gz - 1
            for name, place, count in places:
                for way in (place, count - 1 - place):
                    peers = peers + (way + count - 1) // count
            pl.semaphore_wait(barrier, peers)
            for step in range(1, n_gz):
                owner_copy((g + step) % n_gz).start()
        line_start(CHEB * it, coarse_rhs)
        relaxed(field)
        if it == 0:
            others = owners.at[pl.ds(0, n_gz - 1)]
            pltpu.make_async_copy(others, others, owner_recv_sem).wait()
            blocks[pl.ds(0, 128), :] = b_ref[pl.ds(0, 128), :]
            for k in range(6):
                keep = owners[near_ref[0, k]] == owner_ref[0]
                part = pl.ds((k + 1) * 128, 128)
                blocks[part, :] = jnp.where(keep, b_ref[part, :].astype(F32), 0.0).astype(BF16)

        target = coarse_rhs.astype(F32)
        ratio_now = HALF_WIDTH / CENTRE_VALUE
        direction = target / CENTRE_VALUE
        coarse = direction
        for step in range(CHEB):
            ratio_next = 1.0 / (2.0 * CENTRE_VALUE / HALF_WIDTH - ratio_now)
            turn = CHEB * it + step
            line_finish(turn)
            if step == 0:
                misfit = target - apply_coarse(turn, coarse_rhs) / CENTRE_VALUE
            else:
                misfit = target - apply_coarse(turn, coarse.astype(BF16))
            direction = (
                ratio_next * ratio_now * direction + 2.0 * ratio_next / HALF_WIDTH * misfit
            )
            coarse = coarse + direction
            ratio_now = ratio_next
            if step < CHEB - 1:
                line_start(turn + 1, coarse.astype(BF16))
        coarse = coarse.astype(BF16)

        def correct(j):
            update = smooth[:, cols(j)] + jnp.dot(
                coarse, z_ref[:, cols(j)], preferred_element_type=F32
            )
            smooth[:, cols(j)] = update
            wpad[:, pcols(padded(j))] = row(0, j) * update
            if it == 0:
                sol_ref[:, cols(j)] = update
            else:
                sol_ref[:, cols(j)] = sol_ref[:, cols(j)] + update

        each(0, cy, correct)
        each((cx - 1) * cy, cy, correct)
        for side, x in enumerate((0, cx - 1)):
            xsend[it, side] = wpad[:, pl.ds(((x + 1) * pad_y + 1) * cz, cy * cz)].astype(BF16)
        face_start(it, 0)
        each(cy, (cx - 2) * cy, correct)
        for side, y in enumerate((0, cy - 1)):
            for x in range(cx):
                ysend[it, side, :, pl.ds(x * cz, cz)] = wpad[
                    :, pl.ds(((x + 1) * pad_y + y + 1) * cz, cz)
                ].astype(BF16)
        face_start(it, 1)

        def gather(j, carry):
            low, high = carry
            first = wpad[:, pl.ds(pl.multiple_of(padded(j), 128), 128)]
            last = wpad[:, pl.ds(pl.multiple_of(padded(j) + cz - 128, 128), 128)]
            low = jnp.where(narrow == j, pltpu.roll(first, j, 1), low)
            high = jnp.where(narrow == j, pltpu.roll(last, j + 1, 1), high)
            return low, high

        empty = jnp.zeros((rows, 128), F32)
        low, high = lax.fori_loop(0, cx * cy, gather, (empty, empty))
        zsend[it, 0] = low.astype(BF16)
        zsend[it, 1] = high.astype(BF16)
        face_start(it, 2)

        def apply_inside(j):
            res_ref[:, cols(j)] = (
                field[:, cols(j)]
                - row(1, j) * smooth[:, cols(j)]
                + row(0, j) * beside(padded(j))
            )

        each(0, cx * cy, apply_inside)

        face_wait(it, 2)
        zlow, zhigh = zrecv[it, 0].astype(F32), zrecv[it, 1].astype(F32)

        def add_z(j):
            first = pl.ds(pl.multiple_of(j * cz, 128), 128)
            last = pl.ds(pl.multiple_of(j * cz + cz - 128, 128), 128)
            scale = coef[0, pl.ds(j, 1), :]
            res_ref[:, first] = res_ref[:, first] + jnp.where(
                narrow == 0, scale[:, :128] * pltpu.roll(zlow, (128 - j) % 128, 1), 0.0
            )
            res_ref[:, last] = res_ref[:, last] + jnp.where(
                narrow == 127, scale[:, cz - 128 :] * pltpu.roll(zhigh, 127 - j, 1), 0.0
            )

        each(0, cx * cy, add_z)
        face_wait(it, 1)
        for side, y in enumerate((0, cy - 1)):
            for x in range(cx):
                j = x * cy + y
                part = pl.ds(j * cz, cz)
                res_ref[:, part] = res_ref[:, part] + coef[0, pl.ds(j, 1), :] * yrecv[
                    it, side, :, pl.ds(x * cz, cz)
                ].astype(F32)
        face_wait(it, 0)
        for side, x in enumerate((0, cx - 1)):
            for y in range(cy):
                j = x * cy + y
                part = pl.ds(j * cz, cz)
                res_ref[:, part] = res_ref[:, part] + coef[0, pl.ds(j, 1), :] * xrecv[
                    it, side, :, pl.ds(y * cz, cz)
                ].astype(F32)

    for it in range(ITERS):
        for step in range(CHEB):
            line_drain(CHEB * it + step)
        for which in range(3):
            face_drain(it, which)
    others = owners.at[pl.ds(0, n_gz - 1)]
    pltpu.make_async_copy(others, others, owner_send_sem).wait()


def local(sizes, right_side, stiffness, reaction, deflation, coarse_blocks, row_owner, neighbours):
    n_gx, n_gy, n_gz = sizes
    rows, cx, cy, cz = right_side.shape
    cells = cx * cy * cz
    vectors = deflation.shape[0]
    vmem = pl.BlockSpec(memory_space=pltpu.VMEM)
    smem = pl.BlockSpec(memory_space=pltpu.SMEM)
    turns = ITERS * CHEB
    solution, residual = pl.pallas_call(
        functools.partial(kernel, (n_gx, n_gy, n_gz, cx, cy, cz)),
        out_shape=(jax.ShapeDtypeStruct((rows, cells), F32),) * 2,
        in_specs=[vmem] * 5 + [smem] * 2,
        out_specs=(vmem, vmem),
        scratch_shapes=[
            pltpu.VMEM((4, cx * cy, cz), F32),
            pltpu.VMEM((rows, (cx + 2) * (cy + 2) * cz), F32),
            pltpu.VMEM((rows, cells), F32),
            pltpu.VMEM((7 * vectors, vectors), BF16),
            pltpu.VMEM((n_gz, 1, 128), jnp.int32),
            *[pltpu.VMEM((n_gz, rows, vectors), BF16)] * turns,
            pltpu.VMEM((ITERS, 2, rows, cy * cz), BF16),
            pltpu.VMEM((ITERS, 2, rows, cy * cz), BF16),
            pltpu.VMEM((ITERS, 2, rows, cx * cz), BF16),
            pltpu.VMEM((ITERS, 2, rows, cx * cz), BF16),
            pltpu.VMEM((ITERS, 2, rows, 128), BF16),
            pltpu.VMEM((ITERS, 2, rows, 128), BF16),
            pltpu.SemaphoreType.DMA,
            pltpu.SemaphoreType.DMA,
            pltpu.SemaphoreType.DMA((turns, n_gz)),
            pltpu.SemaphoreType.DMA((turns, n_gz)),
            pltpu.SemaphoreType.DMA((ITERS, 3, 2)),
            pltpu.SemaphoreType.DMA((ITERS, 3, 2)),
        ],
        compiler_params=pltpu.CompilerParams(
            collective_id=0, has_side_effects=True, vmem_limit_bytes=40 * 1024 * 1024
        ),
        name="schwarz",
    )(
        right_side.reshape(rows, cells),
        stiffness.reshape(cx * cy, cz),
        reaction.reshape(cx * cy, cz),
        deflation.reshape(vectors, cells),
        coarse_blocks.reshape(7 * vectors, vectors),
        row_owner,
        neighbours,
    )
    return solution.reshape(right_side.shape), residual.reshape(right_side.shape)


def solution(mesh):
    sizes = tuple(mesh.shape[name] for name in ("gx", "gy", "gz"))
    return jax.shard_map(
        functools.partial(local, sizes),
        mesh=mesh,
        in_specs=(
            P(None, "gx", "gy", "gz"),
            P("gx", "gy", "gz"),
            P("gx", "gy", "gz"),
            P(None, "gx", "gy", "gz"),
            P(("gx", "gy", "gz"), None, None, None),
            P(("gx", "gy", "gz")),
            P(("gx", "gy", "gz"), None),
        ),
        out_specs=(P(None, "gx", "gy", "gz"), P(None, "gx", "gy", "gz")),
        check_vma=False,
    )
```

time: 305 us -> 99 us (0.32)
  the two profiles are of different devices: /device:TPU:25 before, /device:TPU:62 now
where the time goes in v1:
time: 99 us; the launch traced here: 98.7 us
  Pallas kernels  88.3 us (89%)
  local copies, waits for them, and re-layouts  9.07 us (9%)
  between operations  1.35 us (1%)
    pallas_call x1, Pallas kernels, local(): pl.pallas_call(functools.partial(kernel, (n_gx, n_gy, n_gz, cx, cy, cz)),...  88.3 us
    reshape x1, local copies, waits for them, and re-layouts, local(): solution.reshape(right_side.shape)  2.9 us

profile of v1, /device:TPU:62, one launch (start us, length us, event | category | flops | bytes accessed | tf_op | source)
XLA Modules:
  0.0 98.7 jit_solution(526477378673131282)
XLA Ops:
  1.3 0.0 copy-start.4
  1.3 0.7 reshape.26.s_ref
  2.0 0.0 copy-done.4
  2.0 0.0 copy-start.3
  2.1 1.9 %reshape.25.r_ref = f32[64,4096]{1,0:T(8,128)S(1)} reshape(f32[64,4,4,256]{3,2,1,0:T(4,128)} %param.7) | data formatting | bytes 2097152 | tf_op jit(solution)/shard_map/reshape | solution.py:443
  3.9 0.0 copy-done.3
  3.9 0.0 copy-start.1
  3.9 0.0 copy-start.2
  3.9 0.8 reshape.28.z_ref
  4.8 0.1 copy-done.1
  4.9 0.0 copy-done.2
  4.9 88.3 %schwarz.1 = (f32[64,4096]{1,0:T(8,128)S(1)}, f32[64,4096]{1,0:T(8,128)S(1)}) custom-call(f32[64,4096]{1,0:T(8,128)S(1)} %reshape.25.r_ref, f32[16,256]{1,0:T(8,128)S(1)} %reshape.26.s_ref, f32[16,256]{1,0:T(8,128)S(1)} %reshape.27.react_ref, bf16[128,4096]{1,0:T(8,128)(2,1)S(1)} %reshape.28.z_ref, bf16[896,128]{1,0:T(8,128)(2,1)S(1)} %bitcast.1, ...), custom_call_target="tpu_custom_call" | custom-call | tf_op jit(solution)/shard_map/schwarz/pallas_call | solution.py:413
  93.1 0.0 copy-start
  93.1 1.0 copy-done
  94.1 2.9 %reshape.30 = f32[64,4,4,256]{3,2,1,0:T(4,128)} reshape(f32[64,4096]{1,0:T(8,128)} %copy-done) | data formatting | bytes 2097152 | tf_op jit(solution)/shard_map/reshape | solution.py:451
  97.0 1.7 %reshape.31 = f32[64,4,4,256]{3,2,1,0:T(4,128)} reshape(f32[64,4096]{1,0:T(8,128)S(1)} %get-tuple-element.5) | data formatting | bytes 2097152 | tf_op jit(solution)/shard_map/reshape | solution.py:451
  (1 shorter events, 0.0 us)
Async XLA Ops:
  1.3 0.7 copy-start.4
  2.0 1.9 %copy-start.3 = (bf16[128,4,4,256]{3,2,1,0:T(4,128)(2,1)S(1)}, bf16[128,4,4,256]{3,2,1,0:T(4,128)(2,1)}, u32[]{:S(2)}) copy-start(bf16[128,4,4,256]{3,2,1,0:T(4,128)(2,1)} %param.10) | copy-start | bytes 3145732
  3.9 0.9 copy-start.1
  3.9 0.9 copy-start.2
  93.1 1.0 copy-start

commit v2 on v1

--- a/solution.py
+++ b/solution.py
@@ -39,6 +39,7 @@
     near_ref,
     sol_ref,
     res_ref,
+    cells_in,
     coef,
     wpad,
     smooth,
@@ -60,9 +61,11 @@
     line_recv_sem,
     face_send_sem,
     face_recv_sem,
+    field_sem,
+    cells_sem,
 ):
     n_gx, n_gy, n_gz, cx, cy, cz = sizes
-    rows = r_ref.shape[0]
+    rows = res_ref.shape[0]
     n_chips = n_gz // 2
     pad_y = cy + 2
     a, b, g = lax.axis_index("gx"), lax.axis_index("gy"), lax.axis_index("gz")
@@ -73,6 +76,26 @@
     def at_line(place):
         return {"gz": place}
 
+    def cells_copy(which, x):
+        source = (s_ref, react_ref)[which]
+        return pltpu.make_async_copy(
+            source.at[x], cells_in.at[which, pl.ds(x * cy, cy), :], cells_sem.at[which, x]
+        )
+
+    def field_copy(x, y):
+        return pltpu.make_async_copy(
+            r_ref.at[:, x, y, :],
+            res_ref.at[:, pl.ds((x * cy + y) * cz, cz)],
+            field_sem.at[x, y],
+        )
+
+    for x in range(cx):
+        for which in range(2):
+            cells_copy(which, x).start()
+    for x in range(cx):
+        for y in range(cy):
+            field_copy(x, y).start()
+
     barrier = pltpu.get_barrier_semaphore()
     for step in range(1, n_gz):
         pl.semaphore_signal(
@@ -93,8 +116,11 @@
                 barrier, inc=1, device_id={name: place + 1}, device_id_type=MESH
             )
 
-    stiff = s_ref[...]
-    diagonal = 6.0 * stiff * stiff + react_ref[...]
+    for x in range(cx):
+        for which in range(2):
+            cells_copy(which, x).wait()
+    stiff = cells_in[0]
+    diagonal = 6.0 * stiff * stiff + cells_in[1]
     relax = RELAX_WEIGHT / diagonal
     coef[0] = stiff
     coef[1] = diagonal
@@ -131,37 +157,44 @@
 
         lax.fori_loop(0, count, step, 0)
 
-    zero_row = jnp.zeros((rows, pad_y * cz), F32)
-    wpad[:, pl.ds(0, pad_y * cz)] = zero_row
-    wpad[:, pl.ds((cx + 1) * pad_y * cz, pad_y * cz)] = zero_row
-    for x in range(cx):
-        wpad[:, pl.ds((x + 1) * pad_y * cz, cz)] = jnp.zeros((rows, cz), F32)
-        wpad[:, pl.ds(((x + 2) * pad_y - 1) * cz, cz)] = jnp.zeros((rows, cz), F32)
-
-    faces = (("gx", a, n_gx, xrecv), ("gy", b, n_gy, yrecv), ("gz", g, n_gz, zrecv))
-    for it in range(ITERS):
-        for name, place, count, recv in faces:
-
-            @pl.when(place == 0)
-            def _():
-                recv[it, 0] = jnp.zeros(recv.shape[2:], recv.dtype)
-
-            @pl.when(place == count - 1)
-            def _():
-                recv[it, 1] = jnp.zeros(recv.shape[2:], recv.dtype)
-
-    def restrict(field):
-        width = cy * cz
+    def clear():
+        zero_row = jnp.zeros((rows, pad_y * cz), F32)
+        wpad[:, pl.ds(0, pad_y * cz)] = zero_row
+        wpad[:, pl.ds((cx + 1) * pad_y * cz, pad_y * cz)] = zero_row
+        for x in range(cx):
+            wpad[:, pl.ds((x + 1) * pad_y * cz, cz)] = jnp.zeros((rows, cz), F32)
+            wpad[:, pl.ds(((x + 2) * pad_y - 1) * cz, cz)] = jnp.zeros((rows, cz), F32)
+
+        faces = (("gx", a, n_gx, xrecv), ("gy", b, n_gy, yrecv), ("gz", g, n_gz, zrecv))
+        for it in range(ITERS):
+            for name, place, count, recv in faces:
+
+                @pl.when(place == 0)
+                def _():
+                    recv[it, 0] = jnp.zeros(recv.shape[2:], recv.dtype)
+
+                @pl.when(place == count - 1)
+                def _():
+                    recv[it, 1] = jnp.zeros(recv.shape[2:], recv.dtype)
+
+    width = cy * cz
+
+    def restrict_layer(values, x):
+        return lax.dot_general(
+            values.astype(BF16),
+            z_ref[:, pl.ds(pl.multiple_of(x * width, width), width)],
+            (((1,), (1,)), ((), ())),
+            preferred_element_type=F32,
+        )
+
+    def restrict(first):
         total = jnp.zeros((rows, z_ref.shape[0]), F32)
         for x in range(cx):
-            part = pl.ds(x * width, width)
-            total = total + lax.dot_general(
-                field[:, part].astype(BF16),
-                z_ref[:, part],
-                (((1,), (1,)), ((), ())),
-                preferred_element_type=F32,
-            )
-        return total.astype(BF16)
+            if first:
+                for y in range(cy):
+                    field_copy(x, y).wait()
+            total = total + restrict_layer(res_ref[:, pl.ds(x * width, width)], x)
+        return total
 
     def line_copy(turn, slot, sem, target):
         return pltpu.make_async_remote_copy(
@@ -211,27 +244,21 @@
         (2, "gz", g, n_gz, zsend, zrecv),
     )
 
-    def face_start(it, which):
+    def face_start(it, which, side):
         axis, name, place, count, send, recv = exchange[which]
-
-        @pl.when(place > 0)
+        target = place - 1 + 2 * side
+
+        @pl.when((target >= 0) & (target < count))
         def _():
-            face_copy(it, axis, 0, send, recv, name, place - 1).start()
-
-        @pl.when(place < count - 1)
+            face_copy(it, axis, side, send, recv, name, target).start()
+
+    def face_wait(it, which, side):
+        axis, name, place, count, send, recv = exchange[which]
+        source = place - 1 + 2 * side
+
+        @pl.when((source >= 0) & (source < count))
         def _():
-            face_copy(it, axis, 1, send, recv, name, place + 1).start()
-
-    def face_wait(it, which):
-        axis, name, place, count, send, recv = exchange[which]
-
-        @pl.when(place > 0)
-        def _():
-            face_copy(it, axis, 1, send, recv, name, place - 1).wait_recv()
-
-        @pl.when(place < count - 1)
-        def _():
-            face_copy(it, axis, 0, send, recv, name, place + 1).wait_recv()
+            face_copy(it, axis, 1 - side, send, recv, name, source).wait_recv()
 
     def face_drain(it, which):
         axis, name, place, count, send, recv = exchange[which]
@@ -272,8 +299,10 @@
 
     owners[g] = jnp.full((1, 128), owner_ref[0], jnp.int32)
     for it in range(ITERS):
-        field = r_ref if it == 0 else res_ref
-        coarse_rhs = restrict(field)
+        field = res_ref
+        if it == 0:
+            coarse_rhs = restrict(True)
+        coarse_rhs = coarse_rhs.astype(BF16)
         if it == 0:
             peers = n_gz - 1
             for name, place, count in places:
@@ -283,6 +312,8 @@
             for step in range(1, n_gz):
                 owner_copy((g + step) % n_gz).start()
         line_start(CHEB * it, coarse_rhs)
+        if it == 0:
+            clear()
         relaxed(field)
         if it == 0:
             others = owners.at[pl.ds(0, n_gz - 1)]
@@ -319,24 +350,30 @@
                 coarse, z_ref[:, cols(j)], preferred_element_type=F32
             )
             smooth[:, cols(j)] = update
-            wpad[:, pcols(padded(j))] = row(0, j) * update
+            scaled = row(0, j) * update
+            wpad[:, pcols(padded(j))] = scaled
             if it == 0:
                 sol_ref[:, cols(j)] = update
             else:
                 sol_ref[:, cols(j)] = sol_ref[:, cols(j)] + update
-
-        each(0, cy, correct)
-        each((cx - 1) * cy, cy, correct)
-        for side, x in enumerate((0, cx - 1)):
-            xsend[it, side] = wpad[:, pl.ds(((x + 1) * pad_y + 1) * cz, cy * cz)].astype(BF16)
-        face_start(it, 0)
+            return scaled
+
+        sides = (a % 2, 1 - a % 2)
+        for side in sides:
+
+            def correct_layer(y):
+                scaled = correct(side * ((cx - 1) * cy) + y)
+                xsend[it, side, :, cols(y)] = scaled.astype(BF16)
+
+            each(0, cy, correct_layer)
+            face_start(it, 0, side)
         each(cy, (cx - 2) * cy, correct)
         for side, y in enumerate((0, cy - 1)):
             for x in range(cx):
                 ysend[it, side, :, pl.ds(x * cz, cz)] = wpad[
                     :, pl.ds(((x + 1) * pad_y + y + 1) * cz, cz)
                 ].astype(BF16)
-        face_start(it, 1)
+            face_start(it, 1, side)
 
         def gather(j, carry):
             low, high = carry
@@ -350,7 +387,8 @@
         low, high = lax.fori_loop(0, cx * cy, gather, (empty, empty))
         zsend[it, 0] = low.astype(BF16)
         zsend[it, 1] = high.astype(BF16)
-        face_start(it, 2)
+        face_start(it, 2, 0)
+        face_start(it, 2, 1)
 
         def apply_inside(j):
             res_ref[:, cols(j)] = (
@@ -361,7 +399,8 @@
 
         each(0, cx * cy, apply_inside)
 
-        face_wait(it, 2)
+        face_wait(it, 2, 0)
+        face_wait(it, 2, 1)
         zlow, zhigh = zrecv[it, 0].astype(F32), zrecv[it, 1].astype(F32)
 
         def add_z(j):
@@ -376,22 +415,27 @@
             )
 
         each(0, cx * cy, add_z)
-        face_wait(it, 1)
         for side, y in enumerate((0, cy - 1)):
+            face_wait(it, 1, side)
             for x in range(cx):
                 j = x * cy + y
                 part = pl.ds(j * cz, cz)
                 res_ref[:, part] = res_ref[:, part] + coef[0, pl.ds(j, 1), :] * yrecv[
                     it, side, :, pl.ds(x * cz, cz)
                 ].astype(F32)
-        face_wait(it, 0)
-        for side, x in enumerate((0, cx - 1)):
+        for turn, side in enumerate((1 - a % 2, a % 2)):
+            if turn == 1 and it < ITERS - 1:
+                coarse_rhs = restrict(False)
+            face_wait(it, 0, side)
+            x = side * (cx - 1)
+            terms = []
             for y in range(cy):
                 j = x * cy + y
-                part = pl.ds(j * cz, cz)
-                res_ref[:, part] = res_ref[:, part] + coef[0, pl.ds(j, 1), :] * xrecv[
-                    it, side, :, pl.ds(y * cz, cz)
-                ].astype(F32)
+                term = row(0, j) * xrecv[it, side, :, pl.ds(y * cz, cz)].astype(F32)
+                res_ref[:, cols(j)] = res_ref[:, cols(j)] + term
+                terms.append(term.astype(BF16))
+            if turn == 1 and it < ITERS - 1:
+                coarse_rhs = coarse_rhs + restrict_layer(jnp.concatenate(terms, axis=1), x)
 
     for it in range(ITERS):
         for step in range(CHEB):
@@ -402,6 +446,25 @@
     pltpu.make_async_copy(others, others, owner_send_sem).wait()
 
 
+def emit(sol_ref, res_ref, sol_out, res_out, sem):
+    rows, cx, cy, cz = sol_out.shape
+    copies = []
+    for which, (source, target) in enumerate(((sol_ref, sol_out), (res_ref, res_out))):
+        for x in range(cx):
+            for y in range(cy):
+                copies.append(
+                    pltpu.make_async_copy(
+                        source.at[:, pl.ds((x * cy + y) * cz, cz)],
+                        target.at[:, x, y, :],
+                        sem.at[which, x, y],
+                    )
+                )
+    for copy in copies:
+        copy.start()
+    for copy in copies:
+        copy.wait()
+
+
 def local(sizes, right_side, stiffness, reaction, deflation, coarse_blocks, row_owner, neighbours):
     n_gx, n_gy, n_gz = sizes
     rows, cx, cy, cz = right_side.shape
@@ -409,13 +472,16 @@
     vectors = deflation.shape[0]
     vmem = pl.BlockSpec(memory_space=pltpu.VMEM)
     smem = pl.BlockSpec(memory_space=pltpu.SMEM)
+    hbm = pl.BlockSpec(memory_space=pl.ANY)
     turns = ITERS * CHEB
+    flat = jax.ShapeDtypeStruct((rows, cells), F32)
     solution, residual = pl.pallas_call(
         functools.partial(kernel, (n_gx, n_gy, n_gz, cx, cy, cz)),
-        out_shape=(jax.ShapeDtypeStruct((rows, cells), F32),) * 2,
-        in_specs=[vmem] * 5 + [smem] * 2,
+        out_shape=(flat, flat),
+        in_specs=[hbm] * 3 + [vmem] * 2 + [smem] * 2,
         out_specs=(vmem, vmem),
         scratch_shapes=[
+            pltpu.VMEM((2, cx * cy, cz), F32),
             pltpu.VMEM((4, cx * cy, cz), F32),
             pltpu.VMEM((rows, (cx + 2) * (cy + 2) * cz), F32),
             pltpu.VMEM((rows, cells), F32),
@@ -434,21 +500,32 @@
             pltpu.SemaphoreType.DMA((turns, n_gz)),
             pltpu.SemaphoreType.DMA((ITERS, 3, 2)),
             pltpu.SemaphoreType.DMA((ITERS, 3, 2)),
+            pltpu.SemaphoreType.DMA((cx, cy)),
+            pltpu.SemaphoreType.DMA((2, cx)),
         ],
         compiler_params=pltpu.CompilerParams(
-            collective_id=0, has_side_effects=True, vmem_limit_bytes=40 * 1024 * 1024
+            collective_id=0, has_side_effects=True, vmem_limit_bytes=28 * 1024 * 1024
         ),
         name="schwarz",
     )(
-        right_side.reshape(rows, cells),
-        stiffness.reshape(cx * cy, cz),
-        reaction.reshape(cx * cy, cz),
+        right_side,
+        stiffness,
+        reaction,
         deflation.reshape(vectors, cells),
         coarse_blocks.reshape(7 * vectors, vectors),
         row_owner,
         neighbours,
     )
-    return solution.reshape(right_side.shape), residual.reshape(right_side.shape)
+    whole = jax.ShapeDtypeStruct(right_side.shape, F32)
+    return pl.pallas_call(
+        emit,
+        out_shape=(whole, whole),
+        in_specs=[vmem, vmem],
+        out_specs=(hbm, hbm),
+        scratch_shapes=[pltpu.SemaphoreType.DMA((2, cx, cy))],
+        compiler_params=pltpu.CompilerParams(vmem_limit_bytes=4 * 1024 * 1024),
+        name="emit",
+    )(solution, residual)
 
 
 def solution(mesh):

time: 99 us -> 92.8 us (0.937)
  the two profiles are of different devices: /device:TPU:62 before, /device:TPU:58 now
where the time goes in v2:
time: 92.8 us; the launch traced here: 92.6 us
  Pallas kernels  89.3 us (96%)
  local copies, waits for them, and re-layouts  1.92 us (2%)
  between operations  1.37 us (1%)
    pallas_call x1, Pallas kernels, local(): pl.pallas_call(functools.partial(kernel, (n_gx, n_gy, n_gz, cx, cy, cz)),...  87.7 us
    reshape x1, local copies, waits for them, and re-layouts, local(): deflation.reshape(vectors, cells)  1.9 us

profile of v2, /device:TPU:58, one launch (start us, length us, event | category | flops | bytes accessed | tf_op | source)
XLA Modules:
  0.0 92.6 jit_solution(11485031364135720241)
XLA Ops:
  1.3 0.0 copy-start
  1.3 0.0 copy-start.1
  1.3 0.0 copy-start.2
  1.3 0.0 copy-start.3
  1.3 0.0 copy-start.4
  1.3 1.9 %reshape.10.z_ref = bf16[128,4096]{1,0:T(8,128)(2,1)S(1)} reshape(bf16[128,4,4,256]{3,2,1,0:T(4,128)(2,1)} %param.10) | data formatting | bytes 2097152 | tf_op jit(solution)/shard_map/reshape | solution.py:514
  3.2 0.0 copy-done
  3.2 0.0 copy-done.1
  3.3 0.0 copy-done.2
  3.3 0.0 copy-done.3
  3.3 0.0 copy-done.4
  3.3 87.7 %schwarz.1 = (f32[64,4096]{1,0:T(8,128)S(1)}, f32[64,4096]{1,0:T(8,128)S(1)}) custom-call(f32[64,4,4,256]{3,2,1,0:T(4,128)S(1)} %copy-done, f32[4,4,256]{2,1,0:T(4,128)S(1)} %copy-done.2, f32[4,4,256]{2,1,0:T(4,128)S(1)} %copy-done.3, bf16[128,4096]{1,0:T(8,128)(2,1)S(1)} %reshape.10.z_ref, bf16[896,128]{1,0:T(8,128)(2,1)S(1)} %bitcast.1, ...), custom_call_target="tpu_custom_call" | custom-call | tf_op jit(solution)/shard_map/schwarz/pallas_call | solution.py:478
  91.0 1.6 %emit.1 = (f32[64,4,4,256]{3,2,1,0:T(4,128)}, f32[64,4,4,256]{3,2,1,0:T(4,128)}) custom-call(f32[64,4096]{1,0:T(8,128)S(1)} %get-tuple-element.4.sol_ref, f32[64,4096]{1,0:T(8,128)S(1)} %get-tuple-element.5.res_ref), custom_call_target="tpu_custom_call" | custom-call | tf_op jit(solution)/shard_map/emit/pallas_call | solution.py:520
Async XLA Ops:
  1.3 2.0 %copy-start = (f32[64,4,4,256]{3,2,1,0:T(4,128)S(1)}, f32[64,4,4,256]{3,2,1,0:T(4,128)}, u32[]{:S(2)}) copy-start(f32[64,4,4,256]{3,2,1,0:T(4,128)} %r_ref.1) | copy-start | bytes 3145732
  1.3 2.0 %copy-start.1 = (bf16[1,7,128,128]{3,2,1,0:T(8,128)(2,1)S(1)}, bf16[1,7,128,128]{3,2,1,0:T(8,128)(2,1)}, u32[]{:S(2)}) copy-start(bf16[1,7,128,128]{3,2,1,0:T(8,128)(2,1)} %param.11) | copy-start | bytes 688132
  1.3 2.0 %copy-start.2 = (f32[4,4,256]{2,1,0:T(4,128)S(1)}, f32[4,4,256]{2,1,0:T(4,128)}, u32[]{:S(2)}) copy-start(f32[4,4,256]{2,1,0:T(4,128)} %s_ref.1) | copy-start | bytes 49156
  1.3 2.0 %copy-start.3 = (f32[4,4,256]{2,1,0:T(4,128)S(1)}, f32[4,4,256]{2,1,0:T(4,128)}, u32[]{:S(2)}) copy-start(f32[4,4,256]{2,1,0:T(4,128)} %react_ref.1) | copy-start | bytes 49156
  1.3 2.0 %copy-start.4 = (s32[1,6]{1,0:T(1,128)S(1)}, s32[1,6]{1,0:T(1,128)}, u32[]{:S(2)}) copy-start(s32[1,6]{1,0:T(1,128)} %near_ref.1) | copy-start | bytes 76

commit v3 on v2

--- a/solution.py
+++ b/solution.py
@@ -13,6 +13,8 @@
 RELAX_WEIGHT = 0.8
 CENTRE_VALUE = 2.0
 HALF_WIDTH = 1.0
+
+STRAIGHT = 640
 
 MESH = pl.DeviceIdType.MESH
 F32 = jnp.float32
@@ -63,6 +65,9 @@
     face_recv_sem,
     field_sem,
     cells_sem,
+    around,
+    around_send_sem,
+    around_recv_sem,
 ):
     n_gx, n_gy, n_gz, cx, cy, cz = sizes
     rows = res_ref.shape[0]
@@ -76,6 +81,11 @@
     def at_line(place):
         return {"gz": place}
 
+    half = n_gx // 2
+    low_far, high_far = half - 1, half
+    is_far = (a - low_far) * (a - high_far) == 0
+    is_edge = a * (a - (n_gx - 1)) == 0
+
     def cells_copy(which, x):
         source = (s_ref, react_ref)[which]
         return pltpu.make_async_copy(
@@ -115,6 +125,15 @@
             pl.semaphore_signal(
                 barrier, inc=1, device_id={name: place + 1}, device_id_type=MESH
             )
+
+    for here, others in ((is_far, (0, n_gx - 1)), (is_edge, (low_far, high_far))):
+
+        @pl.when(here)
+        def _():
+            for other in others:
+                pl.semaphore_signal(
+                    barrier, inc=1, device_id={"gx": other}, device_id_type=MESH
+                )
 
     for x in range(cx):
         for which in range(2):
@@ -244,11 +263,17 @@
         (2, "gz", g, n_gz, zsend, zrecv),
     )
 
+    def touches(which, place, side, other, count):
+        inside = (other >= 0) & (other < count)
+        if which == 0:
+            inside = inside & (place + other != low_far + high_far)
+        return inside
+
     def face_start(it, which, side):
         axis, name, place, count, send, recv = exchange[which]
         target = place - 1 + 2 * side
 
-        @pl.when((target >= 0) & (target < count))
+        @pl.when(touches(which, place, side, target, count))
         def _():
             face_copy(it, axis, side, send, recv, name, target).start()
 
@@ -256,20 +281,88 @@
         axis, name, place, count, send, recv = exchange[which]
         source = place - 1 + 2 * side
 
-        @pl.when((source >= 0) & (source < count))
+        @pl.when(touches(which, place, side, source, count))
         def _():
             face_copy(it, axis, 1 - side, send, recv, name, source).wait_recv()
+
+    straight = pl.ds(0, STRAIGHT)
+    detour = pl.ds(STRAIGHT, cy * cz - STRAIGHT)
+    far_side = a % 2
+    far_place = low_far + high_far - a
+
+    def straight_copy(it):
+        return pltpu.make_async_remote_copy(
+            src_ref=xsend.at[it, far_side, :, straight],
+            dst_ref=xrecv.at[it, 1 - far_side, :, straight],
+            send_sem=face_send_sem.at[it, 0, far_side],
+            recv_sem=face_recv_sem.at[it, 0, 1 - far_side],
+            device_id={"gx": far_place},
+            device_id_type=MESH,
+        )
+
+    def out_copy(it):
+        return pltpu.make_async_remote_copy(
+            src_ref=xsend.at[it, far_side, :, detour],
+            dst_ref=around.at[it],
+            send_sem=around_send_sem.at[it, 0],
+            recv_sem=around_recv_sem.at[it, 0],
+            device_id={"gx": (1 - far_side) * (n_gx - 1)},
+            device_id_type=MESH,
+        )
+
+    def on_copy(it, side, target):
+        return pltpu.make_async_remote_copy(
+            src_ref=around.at[it],
+            dst_ref=xrecv.at[it, side, :, detour],
+            send_sem=around_send_sem.at[it, 1],
+            recv_sem=around_recv_sem.at[it, 1],
+            device_id={"gx": target},
+            device_id_type=MESH,
+        )
+
+    def far_start(it):
+        @pl.when(is_far)
+        def _():
+            out_copy(it).start()
+            straight_copy(it).start()
+
+    def far_forward(it):
+        @pl.when(is_edge)
+        def _():
+            out_copy(it).wait_recv()
+            on_copy(it, a // (n_gx - 1), high_far - a // (n_gx - 1)).start()
+
+    def far_wait(it):
+        @pl.when(is_far)
+        def _():
+            pltpu.make_async_remote_copy(
+                src_ref=xsend.at[it, far_side, :, straight],
+                dst_ref=xrecv.at[it, far_side, :, straight],
+                send_sem=face_send_sem.at[it, 0, far_side],
+                recv_sem=face_recv_sem.at[it, 0, far_side],
+                device_id={"gx": far_place},
+                device_id_type=MESH,
+            ).wait_recv()
+            on_copy(it, far_side, far_place).wait_recv()
+
+    def far_drain(it):
+        @pl.when(is_far)
+        def _():
+            straight_copy(it).wait_send()
+            out_copy(it).wait_send()
+
+        @pl.when(is_edge)
+        def _():
+            on_copy(it, 1, low_far).wait_send()
 
     def face_drain(it, which):
         axis, name, place, count, send, recv = exchange[which]
-
-        @pl.when(place > 0)
-        def _():
-            face_copy(it, axis, 0, send, recv, name, place - 1).wait_send()
-
-        @pl.when(place < count - 1)
-        def _():
-            face_copy(it, axis, 1, send, recv, name, place + 1).wait_send()
+        for side in range(2):
+            target = place - 1 + 2 * side
+
+            @pl.when(touches(which, place, side, target, count))
+            def _():
+                face_copy(it, axis, side, send, recv, name, target).wait_send()
 
     def relaxed(field):
         def scale(j):
@@ -308,6 +401,9 @@
             for name, place, count in places:
                 for way in (place, count - 1 - place):
                     peers = peers + (way + count - 1) // count
+            within = a % half
+            for way in (within, half - 1 - within):
+                peers = peers + 2 * (1 - (way + half - 1) // half)
             pl.semaphore_wait(barrier, peers)
             for step in range(1, n_gz):
                 owner_copy((g + step) % n_gz).start()
@@ -359,7 +455,7 @@
             return scaled
 
         sides = (a % 2, 1 - a % 2)
-        for side in sides:
+        for turn, side in enumerate(sides):
 
             def correct_layer(y):
                 scaled = correct(side * ((cx - 1) * cy) + y)
@@ -367,7 +463,10 @@
 
             each(0, cy, correct_layer)
             face_start(it, 0, side)
+            if turn == 0:
+                far_start(it)
         each(cy, (cx - 2) * cy, correct)
+        far_forward(it)
         for side, y in enumerate((0, cy - 1)):
             for x in range(cx):
                 ysend[it, side, :, pl.ds(x * cz, cz)] = wpad[
@@ -427,6 +526,8 @@
             if turn == 1 and it < ITERS - 1:
                 coarse_rhs = restrict(False)
             face_wait(it, 0, side)
+            if turn == 1:
+                far_wait(it)
             x = side * (cx - 1)
             terms = []
             for y in range(cy):
@@ -438,6 +539,7 @@
                 coarse_rhs = coarse_rhs + restrict_layer(jnp.concatenate(terms, axis=1), x)
 
     for it in range(ITERS):
+        far_drain(it)
         for step in range(CHEB):
             line_drain(CHEB * it + step)
         for which in range(3):
@@ -502,6 +604,9 @@
             pltpu.SemaphoreType.DMA((ITERS, 3, 2)),
             pltpu.SemaphoreType.DMA((cx, cy)),
             pltpu.SemaphoreType.DMA((2, cx)),
+            pltpu.VMEM((ITERS, rows, cy * cz - STRAIGHT), BF16),
+            pltpu.SemaphoreType.DMA((ITERS, 2)),
+            pltpu.SemaphoreType.DMA((ITERS, 2)),
         ],
         compiler_params=pltpu.CompilerParams(
             collective_id=0, has_side_effects=True, vmem_limit_bytes=28 * 1024 * 1024

time: 92.8 us -> 85.3 us (0.919)
  the two profiles are of different devices: /device:TPU:58 before, /device:TPU:24 now
where the time goes in v3:
time: 85.3 us; the launch traced here: 84.7 us
  Pallas kernels  81.4 us (95%)
  local copies, waits for them, and re-layouts  1.92 us (2%)
  between operations  1.37 us (2%)
    pallas_call x1, Pallas kernels, local(): pl.pallas_call(functools.partial(kernel, (n_gx, n_gy, n_gz, cx, cy, cz)),...  79.9 us
    reshape x1, local copies, waits for them, and re-layouts, local(): deflation.reshape(vectors, cells)  1.9 us

profile of v3, /device:TPU:24, one launch (start us, length us, event | category | flops | bytes accessed | tf_op | source)
XLA Modules:
  0.0 84.7 jit_solution(9963343667113999403)
XLA Ops:
  1.3 0.0 copy-start
  1.3 0.0 copy-start.1
  1.3 0.0 copy-start.2
  1.3 0.0 copy-start.3
  1.3 0.0 copy-start.4
  1.3 1.9 %reshape.10.z_ref = bf16[128,4096]{1,0:T(8,128)(2,1)S(1)} reshape(bf16[128,4,4,256]{3,2,1,0:T(4,128)(2,1)} %param.10) | data formatting | bytes 2097152 | tf_op jit(solution)/shard_map/reshape | solution.py:619
  3.2 0.0 copy-done
  3.2 0.0 copy-done.1
  3.3 0.0 copy-done.2
  3.3 0.0 copy-done.3
  3.3 0.0 copy-done.4
  3.3 79.9 %schwarz.1 = (f32[64,4096]{1,0:T(8,128)S(1)}, f32[64,4096]{1,0:T(8,128)S(1)}) custom-call(f32[64,4,4,256]{3,2,1,0:T(4,128)S(1)} %copy-done, f32[4,4,256]{2,1,0:T(4,128)S(1)} %copy-done.2, f32[4,4,256]{2,1,0:T(4,128)S(1)} %copy-done.3, bf16[128,4096]{1,0:T(8,128)(2,1)S(1)} %reshape.10.z_ref, bf16[896,128]{1,0:T(8,128)(2,1)S(1)} %bitcast.1, ...), custom_call_target="tpu_custom_call" | custom-call | tf_op jit(solution)/shard_map/schwarz/pallas_call | solution.py:580
  83.1 1.6 %emit.1 = (f32[64,4,4,256]{3,2,1,0:T(4,128)}, f32[64,4,4,256]{3,2,1,0:T(4,128)}) custom-call(f32[64,4096]{1,0:T(8,128)S(1)} %get-tuple-element.4.sol_ref, f32[64,4096]{1,0:T(8,128)S(1)} %get-tuple-element.5.res_ref), custom_call_target="tpu_custom_call" | custom-call | tf_op jit(solution)/shard_map/emit/pallas_call | solution.py:625
Async XLA Ops:
  1.3 2.0 %copy-start = (f32[64,4,4,256]{3,2,1,0:T(4,128)S(1)}, f32[64,4,4,256]{3,2,1,0:T(4,128)}, u32[]{:S(2)}) copy-start(f32[64,4,4,256]{3,2,1,0:T(4,128)} %r_ref.1) | copy-start | bytes 3145732
  1.3 2.0 %copy-start.1 = (bf16[1,7,128,128]{3,2,1,0:T(8,128)(2,1)S(1)}, bf16[1,7,128,128]{3,2,1,0:T(8,128)(2,1)}, u32[]{:S(2)}) copy-start(bf16[1,7,128,128]{3,2,1,0:T(8,128)(2,1)} %param.11) | copy-start | bytes 688132
  1.3 2.0 %copy-start.2 = (f32[4,4,256]{2,1,0:T(4,128)S(1)}, f32[4,4,256]{2,1,0:T(4,128)}, u32[]{:S(2)}) copy-start(f32[4,4,256]{2,1,0:T(4,128)} %s_ref.1) | copy-start | bytes 49156
  1.3 2.0 %copy-start.3 = (f32[4,4,256]{2,1,0:T(4,128)S(1)}, f32[4,4,256]{2,1,0:T(4,128)}, u32[]{:S(2)}) copy-start(f32[4,4,256]{2,1,0:T(4,128)} %react_ref.1) | copy-start | bytes 49156
  1.3 2.0 %copy-start.4 = (s32[1,6]{1,0:T(1,128)S(1)}, s32[1,6]{1,0:T(1,128)}, u32[]{:S(2)}) copy-start(s32[1,6]{1,0:T(1,128)} %near_ref.1) | copy-start | bytes 76

commit v4 on v3

--- a/solution.py
+++ b/solution.py
@@ -14,7 +14,7 @@
 CENTRE_VALUE = 2.0
 HALF_WIDTH = 1.0
 
-STRAIGHT = 640
+SHARES = (384, 128, 128)
 
 MESH = pl.DeviceIdType.MESH
 F32 = jnp.float32
@@ -83,8 +83,13 @@
 
     half = n_gx // 2
     low_far, high_far = half - 1, half
-    is_far = (a - low_far) * (a - high_far) == 0
-    is_edge = a * (a - (n_gx - 1)) == 0
+    apart = (a - low_far) * (a - high_far)
+    is_far = apart == 0
+    ways, start = [], cy * cz
+    for via, share in zip([0, *range(half - 2, 0, -1)], SHARES):
+        start -= share
+        ways.append((via, pl.ds(start, share), share))
+    straight = pl.ds(0, start)
 
     def cells_copy(which, x):
         source = (s_ref, react_ref)[which]
@@ -126,14 +131,19 @@
                 barrier, inc=1, device_id={name: place + 1}, device_id_type=MESH
             )
 
-    for here, others in ((is_far, (0, n_gx - 1)), (is_edge, (low_far, high_far))):
-
-        @pl.when(here)
-        def _():
-            for other in others:
-                pl.semaphore_signal(
-                    barrier, inc=1, device_id={"gx": other}, device_id_type=MESH
-                )
+    @pl.when(is_far)
+    def _():
+        for other in [*range(low_far), *range(high_far + 1, n_gx)]:
+            pl.semaphore_signal(
+                barrier, inc=1, device_id={"gx": other}, device_id_type=MESH
+            )
+
+    @pl.when(apart > 0)
+    def _():
+        for other in (low_far, high_far):
+            pl.semaphore_signal(
+                barrier, inc=1, device_id={"gx": other}, device_id_type=MESH
+            )
 
     for x in range(cx):
         for which in range(2):
@@ -285,37 +295,37 @@
         def _():
             face_copy(it, axis, 1 - side, send, recv, name, source).wait_recv()
 
-    straight = pl.ds(0, STRAIGHT)
-    detour = pl.ds(STRAIGHT, cy * cz - STRAIGHT)
     far_side = a % 2
     far_place = low_far + high_far - a
 
-    def straight_copy(it):
+    def straight_copy(it, slot):
         return pltpu.make_async_remote_copy(
             src_ref=xsend.at[it, far_side, :, straight],
-            dst_ref=xrecv.at[it, 1 - far_side, :, straight],
+            dst_ref=xrecv.at[it, slot, :, straight],
             send_sem=face_send_sem.at[it, 0, far_side],
-            recv_sem=face_recv_sem.at[it, 0, 1 - far_side],
+            recv_sem=face_recv_sem.at[it, 0, slot],
             device_id={"gx": far_place},
             device_id_type=MESH,
         )
 
-    def out_copy(it):
+    def out_copy(it, way):
+        via, part, share = ways[way]
         return pltpu.make_async_remote_copy(
-            src_ref=xsend.at[it, far_side, :, detour],
-            dst_ref=around.at[it],
-            send_sem=around_send_sem.at[it, 0],
-            recv_sem=around_recv_sem.at[it, 0],
-            device_id={"gx": (1 - far_side) * (n_gx - 1)},
+            src_ref=xsend.at[it, far_side, :, part],
+            dst_ref=around.at[it, :, pl.ds(0, share)],
+            send_sem=around_send_sem.at[it, 0, way],
+            recv_sem=around_recv_sem.at[it, 0, way],
+            device_id={"gx": via + (1 - far_side) * (n_gx - 1 - 2 * via)},
             device_id_type=MESH,
         )
 
-    def on_copy(it, side, target):
+    def on_copy(it, way, slot, target):
+        via, part, share = ways[way]
         return pltpu.make_async_remote_copy(
-            src_ref=around.at[it],
-            dst_ref=xrecv.at[it, side, :, detour],
-            send_sem=around_send_sem.at[it, 1],
-            recv_sem=around_recv_sem.at[it, 1],
+            src_ref=around.at[it, :, pl.ds(0, share)],
+            dst_ref=xrecv.at[it, slot, :, part],
+            send_sem=around_send_sem.at[it, 1, way],
+            recv_sem=around_recv_sem.at[it, 1, way],
             device_id={"gx": target},
             device_id_type=MESH,
         )
@@ -323,37 +333,39 @@
     def far_start(it):
         @pl.when(is_far)
         def _():
-            out_copy(it).start()
-            straight_copy(it).start()
+            for way in range(len(ways)):
+                out_copy(it, way).start()
+            straight_copy(it, 1 - far_side).start()
+
+    def each_via(action):
+        for way, (via, part, share) in enumerate(ways):
+
+            @pl.when((a - via) * (a - (n_gx - 1 - via)) == 0)
+            def _():
+                action(way)
 
     def far_forward(it):
-        @pl.when(is_edge)
-        def _():
-            out_copy(it).wait_recv()
-            on_copy(it, a // (n_gx - 1), high_far - a // (n_gx - 1)).start()
+        def forward(way):
+            out_copy(it, way).wait_recv()
+            on_copy(it, way, a // half, high_far - a // half).start()
+
+        each_via(forward)
 
     def far_wait(it):
         @pl.when(is_far)
         def _():
-            pltpu.make_async_remote_copy(
-                src_ref=xsend.at[it, far_side, :, straight],
-                dst_ref=xrecv.at[it, far_side, :, straight],
-                send_sem=face_send_sem.at[it, 0, far_side],
-                recv_sem=face_recv_sem.at[it, 0, far_side],
-                device_id={"gx": far_place},
-                device_id_type=MESH,
-            ).wait_recv()
-            on_copy(it, far_side, far_place).wait_recv()
+            straight_copy(it, far_side).wait_recv()
+            for way in range(len(ways)):
+                on_copy(it, way, far_side, far_place).wait_recv()
 
     def far_drain(it):
         @pl.when(is_far)
         def _():
-            straight_copy(it).wait_send()
-            out_copy(it).wait_send()
-
-        @pl.when(is_edge)
-        def _():
-            on_copy(it, 1, low_far).wait_send()
+            straight_copy(it, 1 - far_side).wait_send()
+            for way in range(len(ways)):
+                out_copy(it, way).wait_send()
+
+        each_via(lambda way: on_copy(it, way, a // half, high_far - a // half).wait_send())
 
     def face_drain(it, which):
         axis, name, place, count, send, recv = exchange[which]
@@ -401,9 +413,8 @@
             for name, place, count in places:
                 for way in (place, count - 1 - place):
                     peers = peers + (way + count - 1) // count
-            within = a % half
-            for way in (within, half - 1 - within):
-                peers = peers + 2 * (1 - (way + half - 1) // half)
+            most = n_gx * n_gx
+            peers = peers + 2 + (n_gx - 4) * (1 - (apart + most - 1) // most)
             pl.semaphore_wait(barrier, peers)
             for step in range(1, n_gz):
                 owner_copy((g + step) % n_gz).start()
@@ -604,9 +615,9 @@
             pltpu.SemaphoreType.DMA((ITERS, 3, 2)),
             pltpu.SemaphoreType.DMA((cx, cy)),
             pltpu.SemaphoreType.DMA((2, cx)),
-            pltpu.VMEM((ITERS, rows, cy * cz - STRAIGHT), BF16),
-            pltpu.SemaphoreType.DMA((ITERS, 2)),
-            pltpu.SemaphoreType.DMA((ITERS, 2)),
+            pltpu.VMEM((ITERS, rows, max(SHARES)), BF16),
+            pltpu.SemaphoreType.DMA((ITERS, 2, len(SHARES))),
+            pltpu.SemaphoreType.DMA((ITERS, 2, len(SHARES))),
         ],
         compiler_params=pltpu.CompilerParams(
             collective_id=0, has_side_effects=True, vmem_limit_bytes=28 * 1024 * 1024

time: 85.3 us -> 83.6 us (0.980)
  Pallas kernels: 81.4 us -> 80 us
    pallas_call x1, Pallas kernels: 79.9 us -> 78.4 us  [local(): pl.pallas_call(functools.partial(kernel, (n_gx, n_gy, n_gz, cx, cy, cz)),...]
where the time goes in v4:
time: 83.6 us; the launch traced here: 83.3 us
  Pallas kernels  80 us (96%)
  local copies, waits for them, and re-layouts  1.92 us (2%)
  between operations  1.37 us (2%)
    pallas_call x1, Pallas kernels, local(): pl.pallas_call(functools.partial(kernel, (n_gx, n_gy, n_gz, cx, cy, cz)),...  78.4 us
    reshape x1, local copies, waits for them, and re-layouts, local(): deflation.reshape(vectors, cells)  1.9 us

profile of v4, /device:TPU:24, one launch (start us, length us, event | category | flops | bytes accessed | tf_op | source)
XLA Modules:
  0.0 83.3 jit_solution(7572961391390839302)
XLA Ops:
  1.3 0.0 copy-start
  1.3 0.0 copy-start.1
  1.3 0.0 copy-start.2
  1.3 0.0 copy-start.3
  1.3 0.0 copy-start.4
  1.3 1.9 %reshape.10.z_ref = bf16[128,4096]{1,0:T(8,128)(2,1)S(1)} reshape(bf16[128,4,4,256]{3,2,1,0:T(4,128)(2,1)} %param.10) | data formatting | bytes 2097152 | tf_op jit(solution)/shard_map/reshape | solution.py:630
  3.2 0.0 copy-done
  3.2 0.0 copy-done.1
  3.3 0.0 copy-done.2
  3.3 0.0 copy-done.3
  3.3 0.0 copy-done.4
  3.3 78.4 %schwarz.1 = (f32[64,4096]{1,0:T(8,128)S(1)}, f32[64,4096]{1,0:T(8,128)S(1)}) custom-call(f32[64,4,4,256]{3,2,1,0:T(4,128)S(1)} %copy-done, f32[4,4,256]{2,1,0:T(4,128)S(1)} %copy-done.2, f32[4,4,256]{2,1,0:T(4,128)S(1)} %copy-done.3, bf16[128,4096]{1,0:T(8,128)(2,1)S(1)} %reshape.10.z_ref, bf16[896,128]{1,0:T(8,128)(2,1)S(1)} %bitcast.1, ...), custom_call_target="tpu_custom_call" | custom-call | tf_op jit(solution)/shard_map/schwarz/pallas_call | solution.py:591
  81.7 1.6 %emit.1 = (f32[64,4,4,256]{3,2,1,0:T(4,128)}, f32[64,4,4,256]{3,2,1,0:T(4,128)}) custom-call(f32[64,4096]{1,0:T(8,128)S(1)} %get-tuple-element.4.sol_ref, f32[64,4096]{1,0:T(8,128)S(1)} %get-tuple-element.5.res_ref), custom_call_target="tpu_custom_call" | custom-call | tf_op jit(solution)/shard_map/emit/pallas_call | solution.py:636
Async XLA Ops:
  1.3 2.0 %copy-start = (f32[64,4,4,256]{3,2,1,0:T(4,128)S(1)}, f32[64,4,4,256]{3,2,1,0:T(4,128)}, u32[]{:S(2)}) copy-start(f32[64,4,4,256]{3,2,1,0:T(4,128)} %r_ref.1) | copy-start | bytes 3145732
  1.3 2.0 %copy-start.1 = (bf16[1,7,128,128]{3,2,1,0:T(8,128)(2,1)S(1)}, bf16[1,7,128,128]{3,2,1,0:T(8,128)(2,1)}, u32[]{:S(2)}) copy-start(bf16[1,7,128,128]{3,2,1,0:T(8,128)(2,1)} %param.11) | copy-start | bytes 688132
  1.3 2.0 %copy-start.2 = (f32[4,4,256]{2,1,0:T(4,128)S(1)}, f32[4,4,256]{2,1,0:T(4,128)}, u32[]{:S(2)}) copy-start(f32[4,4,256]{2,1,0:T(4,128)} %s_ref.1) | copy-start | bytes 49156
  1.3 2.0 %copy-start.3 = (f32[4,4,256]{2,1,0:T(4,128)S(1)}, f32[4,4,256]{2,1,0:T(4,128)}, u32[]{:S(2)}) copy-start(f32[4,4,256]{2,1,0:T(4,128)} %react_ref.1) | copy-start | bytes 49156
  1.3 2.0 %copy-start.4 = (s32[1,6]{1,0:T(1,128)S(1)}, s32[1,6]{1,0:T(1,128)}, u32[]{:S(2)}) copy-start(s32[1,6]{1,0:T(1,128)} %near_ref.1) | copy-start | bytes 76

commit v5 on v4

--- a/solution.py
+++ b/solution.py
@@ -104,33 +104,7 @@
             field_sem.at[x, y],
         )
 
-    for x in range(cx):
-        for which in range(2):
-            cells_copy(which, x).start()
-    for x in range(cx):
-        for y in range(cy):
-            field_copy(x, y).start()
-
     barrier = pltpu.get_barrier_semaphore()
-    for step in range(1, n_gz):
-        pl.semaphore_signal(
-            barrier, inc=1, device_id=at_line((g + step) % n_gz), device_id_type=MESH
-        )
-    places = (("gx", a, n_gx), ("gy", b, n_gy))
-    for name, place, count in places:
-
-        @pl.when(place > 0)
-        def _():
-            pl.semaphore_signal(
-                barrier, inc=1, device_id={name: place - 1}, device_id_type=MESH
-            )
-
-        @pl.when(place < count - 1)
-        def _():
-            pl.semaphore_signal(
-                barrier, inc=1, device_id={name: place + 1}, device_id_type=MESH
-            )
-
     @pl.when(is_far)
     def _():
         for other in [*range(low_far), *range(high_far + 1, n_gx)]:
@@ -145,16 +119,43 @@
                 barrier, inc=1, device_id={"gx": other}, device_id_type=MESH
             )
 
+    for step in range(1, n_gz):
+        pl.semaphore_signal(
+            barrier, inc=1, device_id=at_line((g + step) % n_gz), device_id_type=MESH
+        )
+    places = (("gx", a, n_gx), ("gy", b, n_gy))
+    for name, place, count in places:
+
+        @pl.when(place > 0)
+        def _():
+            pl.semaphore_signal(
+                barrier, inc=1, device_id={name: place - 1}, device_id_type=MESH
+            )
+
+        @pl.when(place < count - 1)
+        def _():
+            pl.semaphore_signal(
+                barrier, inc=1, device_id={name: place + 1}, device_id_type=MESH
+            )
+
+    for x in range(cx):
+        for y in range(cy):
+            field_copy(x, y).start()
     for x in range(cx):
         for which in range(2):
-            cells_copy(which, x).wait()
-    stiff = cells_in[0]
-    diagonal = 6.0 * stiff * stiff + cells_in[1]
-    relax = RELAX_WEIGHT / diagonal
-    coef[0] = stiff
-    coef[1] = diagonal
-    coef[2] = (2.0 - RELAX_WEIGHT) * relax
-    coef[3] = stiff * relax
+            cells_copy(which, x).start()
+
+    def coefficients():
+        for x in range(cx):
+            for which in range(2):
+                cells_copy(which, x).wait()
+        stiff = cells_in[0]
+        diagonal = 6.0 * stiff * stiff + cells_in[1]
+        relax = RELAX_WEIGHT / diagonal
+        coef[0] = stiff
+        coef[1] = diagonal
+        coef[2] = (2.0 - RELAX_WEIGHT) * relax
+        coef[3] = stiff * relax
 
     lane = lax.broadcasted_iota(jnp.int32, (rows, cz), 1)
     narrow = lax.broadcasted_iota(jnp.int32, (rows, 128), 1)
@@ -420,6 +421,7 @@
                 owner_copy((g + step) % n_gz).start()
         line_start(CHEB * it, coarse_rhs)
         if it == 0:
+            coefficients()
             clear()
         relaxed(field)
         if it == 0:

time: 83.6 us -> 82.3 us (0.984)
  Pallas kernels: 80 us -> 78.3 us
    pallas_call x1, Pallas kernels: 78.4 us -> 76.7 us  [local(): pl.pallas_call(functools.partial(kernel, (n_gx, n_gy, n_gz, cx, cy, cz)),...]
where the time goes in v5:
time: 82.3 us; the launch traced here: 81.6 us
  Pallas kernels  78.3 us (95%)
  local copies, waits for them, and re-layouts  1.92 us (2%)
  between operations  1.37 us (2%)
    pallas_call x1, Pallas kernels, local(): pl.pallas_call(functools.partial(kernel, (n_gx, n_gy, n_gz, cx, cy, cz)),...  76.7 us
    reshape x1, local copies, waits for them, and re-layouts, local(): deflation.reshape(vectors, cells)  1.9 us

profile of v5, /device:TPU:24, one launch (start us, length us, event | category | flops | bytes accessed | tf_op | source)
XLA Modules:
  0.0 81.6 jit_solution(10595855527723159013)
XLA Ops:
  1.3 0.0 copy-start
  1.3 0.0 copy-start.1
  1.3 0.0 copy-start.2
  1.3 0.0 copy-start.3
  1.3 0.0 copy-start.4
  1.3 1.9 %reshape.10.z_ref = bf16[128,4096]{1,0:T(8,128)(2,1)S(1)} reshape(bf16[128,4,4,256]{3,2,1,0:T(4,128)(2,1)} %param.10) | data formatting | bytes 2097152 | tf_op jit(solution)/shard_map/reshape | solution.py:632
  3.2 0.0 copy-done
  3.2 0.0 copy-done.1
  3.3 0.0 copy-done.2
  3.3 0.0 copy-done.3
  3.3 0.0 copy-done.4
  3.3 76.7 %schwarz.1 = (f32[64,4096]{1,0:T(8,128)S(1)}, f32[64,4096]{1,0:T(8,128)S(1)}) custom-call(f32[64,4,4,256]{3,2,1,0:T(4,128)S(1)} %copy-done, f32[4,4,256]{2,1,0:T(4,128)S(1)} %copy-done.2, f32[4,4,256]{2,1,0:T(4,128)S(1)} %copy-done.3, bf16[128,4096]{1,0:T(8,128)(2,1)S(1)} %reshape.10.z_ref, bf16[896,128]{1,0:T(8,128)(2,1)S(1)} %bitcast.1, ...), custom_call_target="tpu_custom_call" | custom-call | tf_op jit(solution)/shard_map/schwarz/pallas_call | solution.py:593
  80.0 1.6 %emit.1 = (f32[64,4,4,256]{3,2,1,0:T(4,128)}, f32[64,4,4,256]{3,2,1,0:T(4,128)}) custom-call(f32[64,4096]{1,0:T(8,128)S(1)} %get-tuple-element.4.sol_ref, f32[64,4096]{1,0:T(8,128)S(1)} %get-tuple-element.5.res_ref), custom_call_target="tpu_custom_call" | custom-call | tf_op jit(solution)/shard_map/emit/pallas_call | solution.py:638
Async XLA Ops:
  1.3 2.0 %copy-start = (f32[64,4,4,256]{3,2,1,0:T(4,128)S(1)}, f32[64,4,4,256]{3,2,1,0:T(4,128)}, u32[]{:S(2)}) copy-start(f32[64,4,4,256]{3,2,1,0:T(4,128)} %r_ref.1) | copy-start | bytes 3145732
  1.3 2.0 %copy-start.1 = (bf16[1,7,128,128]{3,2,1,0:T(8,128)(2,1)S(1)}, bf16[1,7,128,128]{3,2,1,0:T(8,128)(2,1)}, u32[]{:S(2)}) copy-start(bf16[1,7,128,128]{3,2,1,0:T(8,128)(2,1)} %param.11) | copy-start | bytes 688132
  1.3 2.0 %copy-start.2 = (f32[4,4,256]{2,1,0:T(4,128)S(1)}, f32[4,4,256]{2,1,0:T(4,128)}, u32[]{:S(2)}) copy-start(f32[4,4,256]{2,1,0:T(4,128)} %s_ref.1) | copy-start | bytes 49156
  1.3 2.0 %copy-start.3 = (f32[4,4,256]{2,1,0:T(4,128)S(1)}, f32[4,4,256]{2,1,0:T(4,128)}, u32[]{:S(2)}) copy-start(f32[4,4,256]{2,1,0:T(4,128)} %react_ref.1) | copy-start | bytes 49156
  1.3 2.0 %copy-start.4 = (s32[1,6]{1,0:T(1,128)S(1)}, s32[1,6]{1,0:T(1,128)}, u32[]{:S(2)}) copy-start(s32[1,6]{1,0:T(1,128)} %near_ref.1) | copy-start | bytes 76

commit v6 on v5

--- a/solution.py
+++ b/solution.py
@@ -417,9 +417,10 @@
             most = n_gx * n_gx
             peers = peers + 2 + (n_gx - 4) * (1 - (apart + most - 1) // most)
             pl.semaphore_wait(barrier, peers)
+        line_start(CHEB * it, coarse_rhs)
+        if it == 0:
             for step in range(1, n_gz):
                 owner_copy((g + step) % n_gz).start()
-        line_start(CHEB * it, coarse_rhs)
         if it == 0:
             coefficients()
             clear()
@@ -474,7 +475,8 @@
                 scaled = correct(side * ((cx - 1) * cy) + y)
                 xsend[it, side, :, cols(y)] = scaled.astype(BF16)
 
-            each(0, cy, correct_layer)
+            for y in range(cy):
+                correct_layer(y)
             face_start(it, 0, side)
             if turn == 0:
                 far_start(it)

time: 82.3 us -> 84.7 us (1.029)
  Pallas kernels: 78.3 us -> 81.3 us
    pallas_call x1, Pallas kernels: 76.7 us -> 79.7 us  [local(): pl.pallas_call(functools.partial(kernel, (n_gx, n_gy, n_gz, cx, cy, cz)),...]
where the time goes in v6:
time: 84.7 us; the launch traced here: 84.6 us
  Pallas kernels  81.3 us (96%)
  local copies, waits for them, and re-layouts  1.92 us (2%)
  between operations  1.37 us (2%)
    pallas_call x1, Pallas kernels, local(): pl.pallas_call(functools.partial(kernel, (n_gx, n_gy, n_gz, cx, cy, cz)),...  79.7 us
    reshape x1, local copies, waits for them, and re-layouts, local(): deflation.reshape(vectors, cells)  1.9 us

profile of v6, /device:TPU:24, one launch (start us, length us, event | category | flops | bytes accessed | tf_op | source)
XLA Modules:
  0.0 84.6 jit_solution(17946640307819672198)
XLA Ops:
  1.3 0.0 copy-start
  1.3 0.0 copy-start.1
  1.3 0.0 copy-start.2
  1.3 0.0 copy-start.3
  1.3 0.0 copy-start.4
  1.3 1.9 %reshape.10.z_ref = bf16[128,4096]{1,0:T(8,128)(2,1)S(1)} reshape(bf16[128,4,4,256]{3,2,1,0:T(4,128)(2,1)} %param.10) | data formatting | bytes 2097152 | tf_op jit(solution)/shard_map/reshape | solution.py:634
  3.2 0.0 copy-done
  3.2 0.0 copy-done.1
  3.3 0.0 copy-done.2
  3.3 0.0 copy-done.3
  3.3 0.0 copy-done.4
  3.3 79.7 %schwarz.1 = (f32[64,4096]{1,0:T(8,128)S(1)}, f32[64,4096]{1,0:T(8,128)S(1)}) custom-call(f32[64,4,4,256]{3,2,1,0:T(4,128)S(1)} %copy-done, f32[4,4,256]{2,1,0:T(4,128)S(1)} %copy-done.2, f32[4,4,256]{2,1,0:T(4,128)S(1)} %copy-done.3, bf16[128,4096]{1,0:T(8,128)(2,1)S(1)} %reshape.10.z_ref, bf16[896,128]{1,0:T(8,128)(2,1)S(1)} %bitcast.1, ...), custom_call_target="tpu_custom_call" | custom-call | tf_op jit(solution)/shard_map/schwarz/pallas_call | solution.py:595
  83.0 1.6 %emit.1 = (f32[64,4,4,256]{3,2,1,0:T(4,128)}, f32[64,4,4,256]{3,2,1,0:T(4,128)}) custom-call(f32[64,4096]{1,0:T(8,128)S(1)} %get-tuple-element.4.sol_ref, f32[64,4096]{1,0:T(8,128)S(1)} %get-tuple-element.5.res_ref), custom_call_target="tpu_custom_call" | custom-call | tf_op jit(solution)/shard_map/emit/pallas_call | solution.py:640
Async XLA Ops:
  1.3 2.0 %copy-start = (f32[64,4,4,256]{3,2,1,0:T(4,128)S(1)}, f32[64,4,4,256]{3,2,1,0:T(4,128)}, u32[]{:S(2)}) copy-start(f32[64,4,4,256]{3,2,1,0:T(4,128)} %r_ref.1) | copy-start | bytes 3145732
  1.3 2.0 %copy-start.1 = (bf16[1,7,128,128]{3,2,1,0:T(8,128)(2,1)S(1)}, bf16[1,7,128,128]{3,2,1,0:T(8,128)(2,1)}, u32[]{:S(2)}) copy-start(bf16[1,7,128,128]{3,2,1,0:T(8,128)(2,1)} %param.11) | copy-start | bytes 688132
  1.3 2.0 %copy-start.2 = (f32[4,4,256]{2,1,0:T(4,128)S(1)}, f32[4,4,256]{2,1,0:T(4,128)}, u32[]{:S(2)}) copy-start(f32[4,4,256]{2,1,0:T(4,128)} %s_ref.1) | copy-start | bytes 49156
  1.3 2.0 %copy-start.3 = (f32[4,4,256]{2,1,0:T(4,128)S(1)}, f32[4,4,256]{2,1,0:T(4,128)}, u32[]{:S(2)}) copy-start(f32[4,4,256]{2,1,0:T(4,128)} %react_ref.1) | copy-start | bytes 49156
  1.3 2.0 %copy-start.4 = (s32[1,6]{1,0:T(1,128)S(1)}, s32[1,6]{1,0:T(1,128)}, u32[]{:S(2)}) copy-start(s32[1,6]{1,0:T(1,128)} %near_ref.1) | copy-start | bytes 76
